TPU v7x, 32 devices: a whole 2x2x4 slice. The times are simulated.
32 devices in a mesh: ctx: 16 (over z, x, core), exp: 2 (over y).
Axes of the slice: x: 2, y: 2, z: 4, core: 2. Of those that a mesh axis runs over, the one named last changes fastest.
Arguments:
- feature_in: bfloat16 [6144, 4096], P('ctx', 'exp'), may hold values from -6 to 6
- grad_out: bfloat16 [6144, 4096], P('ctx', 'exp'), may hold values from -6 to 6
- delta: float32 [64, 6144], P('exp', 'ctx'), may hold values from 0.5 to 2
- decay_log: float32 [64], P('exp'), may hold values from -13 to -2
- skip_gain: float32 [64], P('exp'), may hold values from 0.5 to 1.5
- b_proj: float32 [6144, 128], P('ctx'), may hold values from -0.0625 to 0.0625
- c_proj: float32 [6144, 128], P('ctx'), may hold values from -6 to 6
- route_ids: int32 [6144, 4], P('ctx'), may hold values from 0 to 7, all different within a row; in each aligned block of 384 rows (0 to 383, 384 to 767, ...) at most 240 rows name the same one
- route_probs: float32 [6144, 4], P('ctx'), may hold values from 0.05 to 0.5
- w_down: bfloat16 [8, 384, 4096], P('exp'), may hold values from -0.3125 to 0.3125
- saved_act: bfloat16 [16, 8, 240, 384], P('ctx', 'exp'), may hold values from -0.75 to 0.75
Outputs:
- grad_x: bfloat16 [6144, 4096], P('ctx', 'exp')
- grad_delta: float32 [64, 6144], P('exp', 'ctx')
- grad_b: float32 [6144, 128], P(('ctx', 'exp'))
- grad_c: float32 [6144, 128], P(('ctx', 'exp'))
- grad_act: bfloat16 [16, 8, 240, 384], P('ctx', 'exp')
- grad_slots: float32 [16, 8, 240], P('ctx', 'exp')
Inputs may be any that keep to these rules, and one draw needn't show every extreme that they name: `route_ids`: each row names 4 different experts; among the rows of one context shard no expert is named more than 240 times, a bound that some block reaches.
All inputs are finite; a program needn't handle non-finite values.
Results may differ from a plain program's by a relative error of at most 0.0049.
Values may be sent and summed in bfloat16 or wider, within the bound.
A program may use at most 256 MiB of HBM per device.

v0:
```python
from functools import partial

import jax
import jax.numpy as jnp
from jax import lax
from jax.sharding import PartitionSpec as P

HEAD_DIM = 64
EXPERTS = 8
GROUP = 128
CAP = 240


HIGHEST = lax.Precision.HIGHEST


def prefix(value, axis, join, neutral, backward):
    count, mine = (lax.axis_size(axis), lax.axis_index(axis))
    pieces = jax.tree.map(lambda part: lax.all_gather(part, axis), value)
    if backward:
        pieces = jax.tree.map(lambda part: part[::-1], pieces)
        mine = count - 1 - mine
    subtotal = jax.tree.map(
        lambda part, zero: jnp.full_like(part, 0) + jnp.asarray(zero, part.dtype), value, neutral
    )

    def lap(position, subtotal):
        longer = join(subtotal, jax.tree.map(lambda part: part[position], pieces))
        return jax.tree.map(lambda new, old: jnp.where(position < mine, new, old), longer, subtotal)

    return lax.fori_loop(0, count - 1, lap, subtotal)


def block_step(neg_rate, skip_gain, carry_state, pieces):
    inputs, deltas, b_block, c_block = pieces
    block_len = inputs.shape[0]
    logdecay = jnp.cumsum(neg_rate[:, None] * deltas, axis=1)
    gram_mat = jnp.dot(c_block, b_block.T, precision=HIGHEST)
    causal = (
        jnp.arange(block_len, dtype=jnp.int32)[:, None]
        >= jnp.arange(block_len, dtype=jnp.int32)[None, :]
    )
    spread = logdecay[:, :, None] - logdecay[:, None, :]
    weights = jnp.exp(jnp.where(causal[None], spread, -jnp.inf))
    driven = inputs * deltas.T[:, :, None]
    within = jnp.einsum("hts,ts,shp->thp", weights, gram_mat, driven, precision=HIGHEST)
    carried = (
        jnp.einsum("tn,hpn->thp", c_block, carry_state, precision=HIGHEST)
        * jnp.exp(logdecay).T[:, :, None]
    )
    outputs = within + carried + skip_gain[None, :, None] * inputs
    remain = jnp.exp(logdecay[:, -1:] - logdecay)
    updated = jnp.exp(logdecay[:, -1])[:, None, None] * carry_state + jnp.einsum(
        "sn,shp,hs->hpn", b_block, driven, remain, precision=HIGHEST
    )
    return (updated, outputs)


def run_blocks(inputs, deltas, b_full, c_full, start_state, neg_rate, skip_gain, block_len):
    length, head_count, width = inputs.shape
    block_count = length // block_len
    x_blocks = inputs.reshape(block_count, block_len, head_count, width)
    d_blocks = deltas.reshape(head_count, block_count, block_len).transpose(1, 0, 2)
    b_blocks = b_full.reshape(block_count, block_len, -1)
    c_blocks = c_full.reshape(block_count, block_len, -1)
    block_fn = partial(block_step, neg_rate, skip_gain)
    final_state, outputs = lax.scan(block_fn, start_state, (x_blocks, d_blocks, b_blocks, c_blocks))
    return (outputs.reshape(length, head_count, width), final_state)


def link_states(earlier, later):
    return (earlier[0] * later[0], later[0][:, None, None] * earlier[1] + later[1])


def slot_tables(route_ids, route_probs, expert_count, capacity):
    row_count, top_count = route_ids.shape
    flat_ids = route_ids.reshape(-1)
    one_hot = (flat_ids[:, None] == jnp.arange(expert_count, dtype=jnp.int32)[None, :]).astype(
        jnp.int32
    )
    before = jnp.cumsum(one_hot, axis=0) - one_hot
    slot_rank = jnp.sum(before * one_hot, axis=1)
    position = flat_ids * capacity + slot_rank
    token_row = jnp.arange(row_count * top_count, dtype=jnp.int32) // top_count
    slot_table = (
        jnp.full((expert_count * capacity,), row_count, dtype=jnp.int32).at[position].set(token_row)
    )
    weight = (
        jnp.zeros((expert_count * capacity,), jnp.float32).at[position].set(route_probs.reshape(-1))
    )
    return (slot_table.reshape(expert_count, capacity), weight.reshape(expert_count, capacity))


def per_device(
    feature_in,
    grad_out,
    delta,
    decay_log,
    skip_gain,
    b_proj,
    c_proj,
    route_ids,
    route_probs,
    w_down,
    saved_act,
):
    slot_table, slot_probs = slot_tables(route_ids, route_probs, EXPERTS, CAP)
    local_count = w_down.shape[0]
    first_expert = lax.axis_index("exp") * local_count
    my_probs = lax.dynamic_slice_in_dim(slot_probs, first_expert, local_count, 0)
    padded = jnp.concatenate([grad_out, jnp.zeros((1, grad_out.shape[1]), grad_out.dtype)], axis=0)
    picked = lax.all_to_all(padded[slot_table], "exp", split_axis=0, concat_axis=2, tiled=True)
    out_rows = jnp.einsum("kcf,kfd->kcd", saved_act[0], w_down, preferred_element_type=jnp.float32)
    grad_slots = jnp.sum(picked.astype(jnp.float32) * out_rows, axis=2)
    scaled = (my_probs[:, :, None] * picked.astype(jnp.float32)).astype(jnp.bfloat16)
    grad_act = jnp.einsum(
        "kcd,kfd->kcf", scaled, w_down, preferred_element_type=jnp.float32
    ).astype(jnp.bfloat16)
    neg_rate = -jnp.exp(decay_log)
    head_count = decay_log.shape[0]
    length = feature_in.shape[0]
    inputs = feature_in.astype(jnp.float32).reshape(length, head_count, HEAD_DIM)
    cotangent = grad_out.astype(jnp.float32).reshape(length, head_count, HEAD_DIM)
    logdecay = jnp.cumsum(neg_rate[:, None] * delta, axis=1)
    through = jnp.exp(logdecay[:, -1])
    driven = inputs * delta.T[:, :, None]
    own_state = jnp.einsum(
        "sn,shp,hs->hpn", b_proj, driven, jnp.exp(logdecay[:, -1:] - logdecay), precision=HIGHEST
    )
    weighted = cotangent * jnp.exp(logdecay).T[:, :, None]
    own_grad = jnp.einsum("tn,thp->hpn", c_proj, weighted, precision=HIGHEST)
    identity = (jnp.ones((head_count,), jnp.float32), jnp.zeros_like(own_state))
    state_enter = prefix((through, own_state), "ctx", link_states, identity, False)[1]
    grad_leave = prefix((through, own_grad), "ctx", link_states, identity, True)[1]

    def forward_given(feats, deltas, b_mat, c_mat):
        return run_blocks(feats, deltas, b_mat, c_mat, state_enter, neg_rate, skip_gain, GROUP)

    _, pullback = jax.vjp(forward_given, inputs, delta, b_proj, c_proj)
    grad_feat, grad_delta, grad_b, grad_c = pullback((cotangent, grad_leave))
    grad_b, grad_c = (
        lax.psum_scatter(grad_b, "exp", scatter_dimension=0, tiled=True),
        lax.psum_scatter(grad_c, "exp", scatter_dimension=0, tiled=True),
    )
    grad_x = grad_feat.reshape(length, head_count * HEAD_DIM).astype(jnp.bfloat16)
    return (grad_x, grad_delta, grad_b, grad_c, grad_act[None], grad_slots[None])


def solution(mesh):
    placed = (
        P("ctx", "exp"),
        P("ctx", "exp"),
        P("exp", "ctx"),
        P("exp"),
        P("exp"),
        P("ctx", None),
        P("ctx", None),
        P("ctx", None),
        P("ctx", None),
        P("exp", None, None),
        P("ctx", "exp", None, None),
    )
    return jax.shard_map(
        per_device,
        mesh=mesh,
        in_specs=placed,
        out_specs=(
            P("ctx", "exp"),
            P("exp", "ctx"),
            P(("ctx", "exp"), None),
            P(("ctx", "exp"), None),
            P("ctx", "exp", None, None),
            P("ctx", "exp", None),
        ),
        check_vma=False,
    )
```

profile of v0, /device:TPU:0, one launch (start us, length us, event | category | flops | bytes accessed | tf_op | source)
XLA Modules:
  0.0 565.0 jit_solution(587166642446624898)
XLA Ops:
  10.7 1.9 copy.110
  13.7 3.8 fusion.86
  20.7 3.9 fusion.84
  26.9 2.3 reduce-window.16
  29.8 6.2 %scatter_custom_fusion.1 = s32[1920]{0:T(1024)S(1)} fusion(s32[1536]{0:T(1024)S(1)} %fusion.103, s32[1536]{0:T(1024)S(1)} %add_select_fusion, s32[]{:T(128)} %constant.227.clone.1), kind=kCustom, calls=%fused_computation.178 | custom fusion | bytes 7684 | tf_op jit(solution)/shard_map/scatter | solution.py:86
  36.2 8.7 %gather_fusion = bf16[1920,2048]{1,0:T(8,128)(2,1)} fusion(bf16[385,2048]{1,0:T(8,128)(2,1)S(1)} %concatenate.3, s32[2048]{0:T(1024)S(1)} %pad_clamp_fusion), kind=kCustom, calls=%fused_computation | custom fusion | bytes 15736320 | tf_op jit(solution)/shard_map/gather | solution.py:112
  44.9 6.8 %all-to-all-start = ((bf16[8,240,2048]{2,1,0:T(8,128)(2,1)}), bf16[8,240,2048]{2,1,0:T(8,128)(2,1)}, u32[]{:S(2)}, u32[]{:S(2)}) async-start(bf16[8,240,2048]{2,1,0:T(8,128)(2,1)} %bitcast.571), calls=%async_computation.2 | async-start | bytes 15728640 | tf_op jit(solution)/shard_map/all_to_all | solution.py:112
  52.8 5.5 reshape_reshape.6
  58.2 5.5 reshape_reshape.7
  65.2 36.4 %all-reduce.3 = f32[512]{0:T(512)S(1)} all-reduce(f32[512]{0:T(512)S(1)} %dynamic-update-slice), channel_id=2, replica_groups=mesh['ctx'=16,'exp'=2] {'ctx'}, use_global_device_ids=true, to_apply=%add.3 | all-reduce | flops 512 | bytes 4096
  101.7 4.4 copy.114
  106.3 6.2 %scatter_custom_fusion = f32[1920]{0:T(1024)S(1)} fusion(s32[1536]{0:T(1024)S(1)} %fusion.103, f32[1536]{0:T(1024)S(1)} %reshape.365, f32[]{:T(128)} %constant.218.clone.1), kind=kCustom, calls=%fused_computation.180 | custom fusion | bytes 7684 | tf_op jit(solution)/shard_map/scatter | solution.py:89
  114.8 25.1 %all-to-all-done = bf16[8,240,2048]{2,1,0:T(8,128)(2,1)} async-done(((bf16[8,240,2048]{2,1,0:T(8,128)(2,1)}), bf16[8,240,2048]{2,1,0:T(8,128)(2,1)}, u32[]{:S(2)}, u32[]{:S(2)}) %all-to-all-start) | async-done | bytes 7864352 | tf_op jit(solution)/shard_map/all_to_all | solution.py:112
  139.9 11.0 %convert_bitcast_fusion = f32[2,4,30,8,2048]{4,3,2,1,0:T(8,128)} fusion(bf16[2,4,240,2048]{3,2,1,0:T(8,128)(2,1)} %bitcast.95), kind=kLoop, calls=%fused_computation.129 | loop fusion | flops 3932160 | bytes 23592960
  150.9 14.3 %copy.155 = f32[2,4,30,8,2048]{4,3,0,2,1:T(8,128)} copy(f32[2,4,30,8,2048]{4,3,2,1,0:T(8,128)} %convert_bitcast_fusion) | data formatting | bytes 31457280 | tf_op jit(solution)/shard_map/convert_element_type | solution.py:115
  165.2 12.0 %rev.7 = f32[16,32,64,128]{3,2,1,0:T(8,128)} reverse(f32[16,32,64,128]{3,2,1,0:T(8,128)} %bitcast.572), dimensions={0} | reverse | bytes 33554432 | tf_op jit(solution)/shard_map/rev | solution.py:21
  177.2 22.6 %while.98 = (s32[]{:T(128)}, f32[32,64,128]{2,1,0:T(8,128)S(1)}, s32[]{:T(128)}, f32[16,32]{1,0:T(8,128)S(1)}, f32[16,32,64,128]{3,2,1,0:T(8,128)}) while((s32[]{:T(128)}, f32[32,64,128]{2,1,0:T(8,128)S(1)}, s32[]{:T(128)}, f32[16,32]{1,0:T(8,128)S(1)}, f32[16,32,64,128]{3,2,1,0:T(8,128)}) %tuple.182), condition=%wide.region_3.4_spmd.clone.clone, body=%wide.region_2.3_spmd.clone.sunk.clone | while | flops 1048580 | bytes 3146209 | solution.py:31
  199.8 75.3 %all-gather.8.cloned.1.call-done = f32[512,64,128]{2,1,0:T(8,128)} async-done(((f32[32,64,128]{2,1,0:T(8,128)}), f32[512,64,128]{2,1,0:T(8,128)}) %all-gather.8.cloned.1.call-update) | async-done | bytes 16777232 | tf_op jit(solution)/shard_map/all_gather | solution.py:19
  275.1 22.5 %while.99 = (s32[]{:T(128)}, f32[32,64,128]{2,1,0:T(8,128)S(1)}, s32[]{:T(128)}, f32[16,32]{1,0:T(8,128)S(1)}, f32[16,32,64,128]{3,2,1,0:T(8,128)}) while((s32[]{:T(128)}, f32[32,64,128]{2,1,0:T(8,128)S(1)}, s32[]{:T(128)}, f32[16,32]{1,0:T(8,128)S(1)}, f32[16,32,64,128]{3,2,1,0:T(8,128)}) %tuple.208), condition=%wide.region_5.6_spmd.clone.clone, body=%wide.region_4.5_spmd.clone.sunk.clone | while | flops 1048580 | bytes 3146209 | solution.py:31
  299.0 64.1 %while.97 = (s32[]{:T(128)}, f32[32,64,128]{2,1,0:T(8,128)S(1)}, f32[3,128,128]{1,2,0:T(8,128)}, f32[3,32,128,128]{3,2,1,0:T(8,128)}, f32[3,128,32,1]{1,2,3,0:T(...) while((s32[]{:T(128)}, f32[32,64,128]{2,1,0:T(8,128)S(1)}, ...), condition=%wide.region_8.9_spmd.clone.clone.clone, body=%wide.region_6.8_spmd.clone.clone.sunk.clone | while | flops 835461120 | bytes 16751101 | solution.py:67
  299.0 2.0 fusion.213
  304.6 2.8 convolution_add_fusion.9
  310.6 2.4 multiply_dynamic-update-slice_fusion.3
  317.9 2.4 bitcast_dynamic-update-slice_fusion.31
  320.3 2.0 fusion.213
  325.9 2.8 convolution_add_fusion.9
  331.9 2.4 multiply_dynamic-update-slice_fusion.3
  339.2 2.5 bitcast_dynamic-update-slice_fusion.31
  341.7 2.0 fusion.213
  347.3 2.8 convolution_add_fusion.9
  353.3 2.3 multiply_dynamic-update-slice_fusion.3
  360.7 2.4 bitcast_dynamic-update-slice_fusion.31
  365.1 154.3 %while.96 = (s32[]{:T(128)}, f32[32,64,128]{2,1,0:T(8,128)S(1)}, bf16[3,128,32,64]{1,3,2,0:T(8,128)(2,1)}, f32[3,32,128]{2,1,0:T(8,128)}, f32[3,128,128]{2,1,0:T...) while((s32[]{:T(128)}, f32[32,64,128]{2,1,0:T(8,128)S(1)}, ...), condition=%wide.region_17.18_spmd.clone.clone, body=%wide.region_9.0_spmd.clone.sunk.clone | while | flops 2474946560 | bytes 53224156 | solution.py:67
  376.4 3.7 convolution_bitcast_fusion.7
  380.2 2.1 fusion.203
  382.3 2.2 fusion.198
  384.5 3.4 constant_dynamic-slice_fusion.15
  392.3 3.7 bitcast_dynamic-update-slice_fusion.24
  396.1 3.3 fusion.200
  399.4 6.8 %fusion.201 = (f32[32,128]{1,0:T(8,128)S(1)}, f32[32,128]{1,0:T(8,128)S(1)}, f32[32,128,128]{2,1,0:T(8,128)}) fusion(f32[3,32,128,128]{3,2,1,0:T(8,128)} %get-tuple-element.2249, s32[]{:T(128)S(6)} %sub.161, f32[128,128]{1,0:T(8,128)S(1)} %dynamic-slice_bitcast_fusion.17, pred[128,128]{1,0:T(8,128)(4,1)S(1)} %get-tuple-element.2252, ...), kind=kOutput, calls=%fused_computation.53.clone.1.clone | convolution fusion | flops 405266432 | bytes 6407168 | tf_op jit(solution)/shard_map/transpose(jvp())/while/body/eval_jaxpr/hts,ts,shp->thp/dot_general | solution.py:46
  415.9 2.5 fusion.206
  419.3 3.0 convolution_bitcast_fusion.8
  424.1 3.7 convolution_bitcast_fusion.7
  427.8 2.1 fusion.203
  429.9 2.2 fusion.198
  432.2 3.4 constant_dynamic-slice_fusion.15
  439.9 3.7 bitcast_dynamic-update-slice_fusion.24
  443.6 3.3 fusion.200
  446.9 6.8 %fusion.201 = (f32[32,128]{1,0:T(8,128)S(1)}, f32[32,128]{1,0:T(8,128)S(1)}, f32[32,128,128]{2,1,0:T(8,128)}) fusion(f32[3,32,128,128]{3,2,1,0:T(8,128)} %get-tuple-element.2249, s32[]{:T(128)S(6)} %sub.161, f32[128,128]{1,0:T(8,128)S(1)} %dynamic-slice_bitcast_fusion.17, pred[128,128]{1,0:T(8,128)(4,1)S(1)} %get-tuple-element.2252, ...), kind=kOutput, calls=%fused_computation.53.clone.1.clone | convolution fusion | flops 405266432 | bytes 6407168 | tf_op jit(solution)/shard_map/transpose(jvp())/while/body/eval_jaxpr/hts,ts,shp->thp/dot_general | solution.py:46
  463.5 2.5 fusion.206
  466.9 3.0 convolution_bitcast_fusion.8
  471.6 3.7 convolution_bitcast_fusion.7
  475.4 2.1 fusion.203
  477.5 2.2 fusion.198
  479.7 3.4 constant_dynamic-slice_fusion.15
  487.4 3.7 bitcast_dynamic-update-slice_fusion.24
  491.2 3.3 fusion.200
  494.5 6.8 %fusion.201 = (f32[32,128]{1,0:T(8,128)S(1)}, f32[32,128]{1,0:T(8,128)S(1)}, f32[32,128,128]{2,1,0:T(8,128)}) fusion(f32[3,32,128,128]{3,2,1,0:T(8,128)} %get-tuple-element.2249, s32[]{:T(128)S(6)} %sub.161, f32[128,128]{1,0:T(8,128)S(1)} %dynamic-slice_bitcast_fusion.17, pred[128,128]{1,0:T(8,128)(4,1)S(1)} %get-tuple-element.2252, ...), kind=kOutput, calls=%fused_computation.53.clone.1.clone | convolution fusion | flops 405266432 | bytes 6407168 | tf_op jit(solution)/shard_map/transpose(jvp())/while/body/eval_jaxpr/hts,ts,shp->thp/dot_general | solution.py:46
  511.1 2.5 fusion.206
  514.4 3.0 convolution_bitcast_fusion.8
  519.4 14.8 %fusion.92 = bf16[1,4,240,384]{3,2,1,0:T(8,128)(2,1)} fusion(bf16[4,384,4096]{2,1,0:T(8,128)(2,1)} %param.28, f32[4,240,4096]{2,1,0:T(8,128)} %bitcast.569, f32[4,240]{1,0:T(4,128)} %constant_dynamic-slice_fusion.6), kind=kOutput, calls=%fused_computation.143 | convolution fusion | flops 3028131840 | bytes 29052672 | tf_op jit(solution)/shard_map/kcd,kfd->kcf/dot_general | solution.py:116
  534.3 12.6 %multiply_reduce_fusion = f32[4,240]{1,0:T(4,128)} fusion(f32[4,240,4096]{2,1,0:T(8,128)} %bitcast.570, bf16[4,384,4096]{2,1,0:T(8,128)(2,1)} %param.28, bf16[1,4,240,384]{3,2,1,0:T(8,128)(2,1)S(1)} %copy-done), kind=kOutput, calls=%fused_computation.130 | convolution fusion | flops 3027762176 | bytes 29052672 | tf_op jit(solution)/shard_map/kcf,kfd->kcd/dot_general | solution.py:113
  547.0 5.1 copy.141
  552.0 5.6 reshape.403
  (325 shorter events, 148.8 us)
Async XLA Ops:
  7.2 527.1 %copy-start = (bf16[1,4,240,384]{3,2,1,0:T(8,128)(2,1)S(1)}, bf16[1,4,240,384]{3,2,1,0:T(8,128)(2,1)}, u32[]{:S(2)}) copy-start(bf16[1,4,240,384]{3,2,1,0:T(8,128)(2,1)} %param.29) | copy-start | bytes 2211844
  7.2 158.0 %all-gather.6.cloned.1.call-start = ((), (), s32[]{:S(2)}) async-start(), calls=%async_computation.5 | async-start | bytes 17825792 | tf_op jit(solution)/shard_map/all_gather | solution.py:19
  12.6 5.0 copy-start.1
  12.6 1.1 copy-start.3
  17.5 257.6 %all-gather.8.cloned.1.call-start = ((), (), s32[]{:S(2)}) async-start(), calls=%async_computation.6 | async-start | bytes 17825792 | tf_op jit(solution)/shard_map/all_gather | solution.py:19
  19.5 5.1 copy-start.2
  19.5 1.1 copy-start.4
  19.5 1.2 copy-start.15
  19.7 4.9 copy-start.17
  44.9 95.0 %all-to-all-start = ((bf16[8,240,2048]{2,1,0:T(8,128)(2,1)}), bf16[8,240,2048]{2,1,0:T(8,128)(2,1)}, u32[]{:S(2)}, u32[]{:S(2)}) async-start(bf16[8,240,2048]{2,1,0:T(8,128)(2,1)} %bitcast.571), calls=%async_computation.2 | async-start | bytes 15728640 | tf_op jit(solution)/shard_map/all_to_all | solution.py:112
  51.7 506.6 %reduce-scatter.3.cloned.1.call-start = ((), (), s32[]{:S(2)}) async-start(), calls=%async_computation.3 | async-start | bytes 294912 | tf_op jit(solution)/shard_map/reduce_scatter | solution.py:142
  58.2 5.5 copy-start.20
  101.7 4.4 copy-start.19
  376.4 22.9 %copy-start.13 = (f32[3,128,128]{2,1,0:T(8,128)}, f32[3,128,128]{2,1,0:T(8,128)S(1)}, u32[]{:S(2)}) copy-start(f32[3,128,128]{2,1,0:T(8,128)S(1)} %get-tuple-element.2248) | copy-start | bytes 589828 | tf_op jit(solution)/shard_map/transpose(jvp())/while
  376.4 22.9 %copy-start.9 = (pred[128,128]{1,0:T(8,128)(4,1)}, pred[128,128]{1,0:T(8,128)(4,1)S(1)}, u32[]{:S(2)}) copy-start(pred[128,128]{1,0:T(8,128)(4,1)S(1)} %get-tuple-element.2252) | copy-start | bytes 49156 | tf_op jit(solution)/shard_map/transpose(jvp())/while
  384.5 7.8 %copy-start.6 = (bf16[3,128,32,64]{1,3,2,0:T(8,128)(2,1)S(1)}, bf16[3,128,32,64]{1,3,2,0:T(8,128)(2,1)}, u32[]{:S(2)}) copy-start(bf16[3,128,32,64]{1,3,2,0:T(8,128)(2,1)} %get-tuple-element.2201) | copy-start | bytes 4718596 | tf_op jit(solution)/shard_map/transpose(jvp())/while
  384.5 7.8 %copy-start.18 = (f32[1,32,1]{1,2,0:T(1,128)S(1)}, f32[1,32,1]{1,2,0:T(1,128)}, u32[]{:S(2)}) copy-start(f32[1,32,1]{1,2,0:T(1,128)} %get-tuple-element.2236) | copy-start | bytes 388 | tf_op jit(solution)/shard_map/transpose(jvp())/while
  388.7 7.4 %copy-start.11 = (f32[128,32]{0,1:T(8,128)}, f32[128,32]{0,1:T(8,128)S(1)}, u32[]{:S(2)}) copy-start(f32[128,32]{0,1:T(8,128)S(1)} %dynamic-slice_bitcast_fusion.15) | copy-start | bytes 49156 | tf_op jit(solution)/shard_map/transpose(jvp())/while
  396.1 10.1 %copy-start.7 = (bf16[3,128,32,64]{1,3,2,0:T(8,128)(2,1)}, bf16[3,128,32,64]{1,3,2,0:T(8,128)(2,1)S(1)}, u32[]{:S(2)}) copy-start(bf16[3,128,32,64]{1,3,2,0:T(8,128)(2,1)S(1)} %get-tuple-element.2228) | copy-start | bytes 4718596 | tf_op jit(solution)/shard_map/transpose(jvp())/while
  412.3 6.1 %copy-start.5 = (f32[128,128]{1,0:T(8,128)S(1)}, f32[128,128]{1,0:T(8,128)}, u32[]{:S(2)}) copy-start(f32[128,128]{1,0:T(8,128)} %convolution_bitcast_fusion.7) | copy-start | bytes 196612 | tf_op jit(solution)/shard_map/transpose(jvp())/while
  412.4 7.0 %copy-start.12 = (f32[128,32]{0,1:T(8,128)S(1)}, f32[128,32]{0,1:T(8,128)}, u32[]{:S(2)}) copy-start(f32[128,32]{0,1:T(8,128)} %copy-done.11) | copy-start | bytes 49156 | tf_op jit(solution)/shard_map/transpose(jvp())/while
  415.9 8.1 %copy-start.10 = (pred[128,128]{1,0:T(8,128)(4,1)S(1)}, pred[128,128]{1,0:T(8,128)(4,1)}, u32[]{:S(2)}) copy-start(pred[128,128]{1,0:T(8,128)(4,1)} %copy-done.9) | copy-start | bytes 49156 | tf_op jit(solution)/shard_map/transpose(jvp())/while
  415.9 8.1 %copy-start.14 = (f32[3,128,128]{2,1,0:T(8,128)S(1)}, f32[3,128,128]{2,1,0:T(8,128)}, u32[]{:S(2)}) copy-start(f32[3,128,128]{2,1,0:T(8,128)} %copy-done.13) | copy-start | bytes 589828 | tf_op jit(solution)/shard_map/transpose(jvp())/while
  424.1 22.8 %copy-start.13 = (f32[3,128,128]{2,1,0:T(8,128)}, f32[3,128,128]{2,1,0:T(8,128)S(1)}, u32[]{:S(2)}) copy-start(f32[3,128,128]{2,1,0:T(8,128)S(1)} %get-tuple-element.2248) | copy-start | bytes 589828 | tf_op jit(solution)/shard_map/transpose(jvp())/while
  424.1 22.9 %copy-start.9 = (pred[128,128]{1,0:T(8,128)(4,1)}, pred[128,128]{1,0:T(8,128)(4,1)S(1)}, u32[]{:S(2)}) copy-start(pred[128,128]{1,0:T(8,128)(4,1)S(1)} %get-tuple-element.2252) | copy-start | bytes 49156 | tf_op jit(solution)/shard_map/transpose(jvp())/while
  432.1 7.7 %copy-start.6 = (bf16[3,128,32,64]{1,3,2,0:T(8,128)(2,1)S(1)}, bf16[3,128,32,64]{1,3,2,0:T(8,128)(2,1)}, u32[]{:S(2)}) copy-start(bf16[3,128,32,64]{1,3,2,0:T(8,128)(2,1)} %get-tuple-element.2201) | copy-start | bytes 4718596 | tf_op jit(solution)/shard_map/transpose(jvp())/while
  432.1 7.7 %copy-start.18 = (f32[1,32,1]{1,2,0:T(1,128)S(1)}, f32[1,32,1]{1,2,0:T(1,128)}, u32[]{:S(2)}) copy-start(f32[1,32,1]{1,2,0:T(1,128)} %get-tuple-element.2236) | copy-start | bytes 388 | tf_op jit(solution)/shard_map/transpose(jvp())/while
  436.3 7.3 %copy-start.11 = (f32[128,32]{0,1:T(8,128)}, f32[128,32]{0,1:T(8,128)S(1)}, u32[]{:S(2)}) copy-start(f32[128,32]{0,1:T(8,128)S(1)} %dynamic-slice_bitcast_fusion.15) | copy-start | bytes 49156 | tf_op jit(solution)/shard_map/transpose(jvp())/while
  443.6 10.1 %copy-start.7 = (bf16[3,128,32,64]{1,3,2,0:T(8,128)(2,1)}, bf16[3,128,32,64]{1,3,2,0:T(8,128)(2,1)S(1)}, u32[]{:S(2)}) copy-start(bf16[3,128,32,64]{1,3,2,0:T(8,128)(2,1)S(1)} %get-tuple-element.2228) | copy-start | bytes 4718596 | tf_op jit(solution)/shard_map/transpose(jvp())/while
  459.9 6.1 %copy-start.5 = (f32[128,128]{1,0:T(8,128)S(1)}, f32[128,128]{1,0:T(8,128)}, u32[]{:S(2)}) copy-start(f32[128,128]{1,0:T(8,128)} %convolution_bitcast_fusion.7) | copy-start | bytes 196612 | tf_op jit(solution)/shard_map/transpose(jvp())/while
  459.9 7.0 %copy-start.12 = (f32[128,32]{0,1:T(8,128)S(1)}, f32[128,32]{0,1:T(8,128)}, u32[]{:S(2)}) copy-start(f32[128,32]{0,1:T(8,128)} %copy-done.11) | copy-start | bytes 49156 | tf_op jit(solution)/shard_map/transpose(jvp())/while
  463.5 8.1 %copy-start.10 = (pred[128,128]{1,0:T(8,128)(4,1)S(1)}, pred[128,128]{1,0:T(8,128)(4,1)}, u32[]{:S(2)}) copy-start(pred[128,128]{1,0:T(8,128)(4,1)} %copy-done.9) | copy-start | bytes 49156 | tf_op jit(solution)/shard_map/transpose(jvp())/while
  463.5 8.1 %copy-start.14 = (f32[3,128,128]{2,1,0:T(8,128)S(1)}, f32[3,128,128]{2,1,0:T(8,128)}, u32[]{:S(2)}) copy-start(f32[3,128,128]{2,1,0:T(8,128)} %copy-done.13) | copy-start | bytes 589828 | tf_op jit(solution)/shard_map/transpose(jvp())/while
  471.6 22.9 %copy-start.13 = (f32[3,128,128]{2,1,0:T(8,128)}, f32[3,128,128]{2,1,0:T(8,128)S(1)}, u32[]{:S(2)}) copy-start(f32[3,128,128]{2,1,0:T(8,128)S(1)} %get-tuple-element.2248) | copy-start | bytes 589828 | tf_op jit(solution)/shard_map/transpose(jvp())/while
  471.6 22.9 %copy-start.9 = (pred[128,128]{1,0:T(8,128)(4,1)}, pred[128,128]{1,0:T(8,128)(4,1)S(1)}, u32[]{:S(2)}) copy-start(pred[128,128]{1,0:T(8,128)(4,1)S(1)} %get-tuple-element.2252) | copy-start | bytes 49156 | tf_op jit(solution)/shard_map/transpose(jvp())/while
  479.7 7.8 %copy-start.6 = (bf16[3,128,32,64]{1,3,2,0:T(8,128)(2,1)S(1)}, bf16[3,128,32,64]{1,3,2,0:T(8,128)(2,1)}, u32[]{:S(2)}) copy-start(bf16[3,128,32,64]{1,3,2,0:T(8,128)(2,1)} %get-tuple-element.2201) | copy-start | bytes 4718596 | tf_op jit(solution)/shard_map/transpose(jvp())/while
  479.7 7.8 %copy-start.18 = (f32[1,32,1]{1,2,0:T(1,128)S(1)}, f32[1,32,1]{1,2,0:T(1,128)}, u32[]{:S(2)}) copy-start(f32[1,32,1]{1,2,0:T(1,128)} %get-tuple-element.2236) | copy-start | bytes 388 | tf_op jit(solution)/shard_map/transpose(jvp())/while
  483.9 7.3 %copy-start.11 = (f32[128,32]{0,1:T(8,128)}, f32[128,32]{0,1:T(8,128)S(1)}, u32[]{:S(2)}) copy-start(f32[128,32]{0,1:T(8,128)S(1)} %dynamic-slice_bitcast_fusion.15) | copy-start | bytes 49156 | tf_op jit(solution)/shard_map/transpose(jvp())/while
  491.2 10.0 %copy-start.7 = (bf16[3,128,32,64]{1,3,2,0:T(8,128)(2,1)}, bf16[3,128,32,64]{1,3,2,0:T(8,128)(2,1)S(1)}, u32[]{:S(2)}) copy-start(bf16[3,128,32,64]{1,3,2,0:T(8,128)(2,1)S(1)} %get-tuple-element.2228) | copy-start | bytes 4718596 | tf_op jit(solution)/shard_map/transpose(jvp())/while
  507.5 6.1 %copy-start.5 = (f32[128,128]{1,0:T(8,128)S(1)}, f32[128,128]{1,0:T(8,128)}, u32[]{:S(2)}) copy-start(f32[128,128]{1,0:T(8,128)} %convolution_bitcast_fusion.7) | copy-start | bytes 196612 | tf_op jit(solution)/shard_map/transpose(jvp())/while
  507.5 7.0 %copy-start.12 = (f32[128,32]{0,1:T(8,128)S(1)}, f32[128,32]{0,1:T(8,128)}, u32[]{:S(2)}) copy-start(f32[128,32]{0,1:T(8,128)} %copy-done.11) | copy-start | bytes 49156 | tf_op jit(solution)/shard_map/transpose(jvp())/while
  511.0 8.1 %copy-start.10 = (pred[128,128]{1,0:T(8,128)(4,1)S(1)}, pred[128,128]{1,0:T(8,128)(4,1)}, u32[]{:S(2)}) copy-start(pred[128,128]{1,0:T(8,128)(4,1)} %copy-done.9) | copy-start | bytes 49156 | tf_op jit(solution)/shard_map/transpose(jvp())/while
  511.0 8.1 %copy-start.14 = (f32[3,128,128]{2,1,0:T(8,128)S(1)}, f32[3,128,128]{2,1,0:T(8,128)}, u32[]{:S(2)}) copy-start(f32[3,128,128]{2,1,0:T(8,128)} %copy-done.13) | copy-start | bytes 589828 | tf_op jit(solution)/shard_map/transpose(jvp())/while
  519.4 38.9 %reduce-scatter.5.cloned.1.call-start = ((), (), s32[]{:S(2)}) async-start(), calls=%async_computation.4 | async-start | bytes 294912 | tf_op jit(solution)/shard_map/reduce_scatter | solution.py:143
  534.3 12.6 %copy-start.8 = (bf16[3,128,32,64]{1,3,2,0:T(8,128)(2,1)S(1)}, bf16[3,128,32,64]{1,3,2,0:T(8,128)(2,1)}, u32[]{:S(2)}) copy-start(bf16[3,128,32,64]{1,3,2,0:T(8,128)(2,1)} %get-tuple-element.933) | copy-start | bytes 4718596
  552.0 5.6 copy-start.16
Sparse Core Ops, SparseCore 0:
  17.7 130.1 all-gather.5
  150.0 125.0 all-gather.7
  519.5 9.1 reduce-scatter.2
  534.4 9.1 reduce-scatter.4
where the time goes:
time: 572 us; the launch traced here: 565 us
  local copies, waits for them, and re-layouts  141 us (25%)
  other arithmetic  131 us (23%)
  matrix products  121 us (21%)
  waiting for transfers between devices  101 us (18%)
  blocking collectives  36.4 us (6%)
  between operations  15.1 us (3%)
  loops' own time  12.9 us (2%)
  starting transfers between devices  7.19 us (1%)
    all_gather x2, waiting for transfers between devices, prefix(): pieces = jax.tree.map(lambda part: lax.all_gather(part, axis), value)  75.3 us
    select_n x30, other arithmetic, lap(): jnp.where(position < mine, new, old)  43.9 us
    unnamed x1, blocking collectives  36.4 us
    dot_general x6, matrix products, block_step(): jnp.einsum('hts,ts,shp->thp', weights, gram_mat, driven, precision=HIGHEST)  31.5 us
    dynamic_update_slice x18, other arithmetic, run_blocks(): lax.scan(block_fn, start_state, (x_blocks, d_blocks, b_blocks, c_blocks))  31 us
    dot_general x9, matrix products, block_step(): jnp.einsum('sn,shp,hs->hpn', b_block, driven, remain, precision=HIGHEST)  26.3 us
    all_to_all x1, waiting for transfers between devices, per_device(): lax.all_to_all(padded[slot_table], 'exp', split_axis=0, concat_axis=2, ti...  25.1 us
    dynamic_slice x18, local copies, waits for them, and re-layouts, run_blocks(): lax.scan(block_fn, start_state, (x_blocks, d_blocks, b_blocks, c_blocks))  21.7 us
  transfers between devices with their start and end apart: 5, of which 2 were waited for; matrix products, arithmetic and copies ran while one was open for 27% of the time, Pallas kernels for 0%

commit v1 on v0

v1 whole, which is shorter than its diff:
```python
from functools import partial

import jax
import jax.numpy as jnp
from jax import lax
from jax.experimental import pallas as pl
from jax.experimental.pallas import tpu as pltpu
from jax.sharding import PartitionSpec as P

HEAD_DIM = 64
CHUNK = 128
LANES = 128
HIGHEST = lax.Precision.HIGHEST
F32 = jnp.float32
BF16 = jnp.bfloat16
MESH = pl.DeviceIdType.MESH


def nn(a, b, precision=None):
    return lax.dot_general(
        a, b, (((1,), (0,)), ((), ())), precision=precision, preferred_element_type=F32
    )


def nt(a, b, precision=None):
    return lax.dot_general(
        a, b, (((1,), (1,)), ((), ())), precision=precision, preferred_element_type=F32
    )


def split(value, count):
    parts = []
    for _ in range(count):
        part = value.astype(BF16)
        parts.append(part)
        value = value - part.astype(F32)
    return parts


def spread_out(parts, chosen):
    total = nn(parts[0], chosen)
    for part in parts[1:]:
        total = total + nn(part, chosen)
    return total


def iota(shape, dim):
    return lax.broadcasted_iota(jnp.int32, shape, dim)


def head_lanes(heads, width, first):
    return (iota((heads, width), 0) == first + iota((heads, width), 1) // HEAD_DIM).astype(BF16)


def chain_kernel(
    n_ctx, n_exp, pieces,
    x_ref, g_ref, g_any, delta_t_ref, rate_ref, b_t_ref, c_t_ref,
    g_full, enter_ref, leave_ref,
    own_f, own_b, in_f, in_b, out_f, out_b, through_ref,
    send_f, recv_f, send_b, recv_b, send_g, recv_g, local_sem,
):
    me, side = lax.axis_index("ctx"), lax.axis_index("exp")
    right, left = lax.rem(me + 1, n_ctx), lax.rem(me + n_ctx - 1, n_ctx)
    barrier = pltpu.get_barrier_semaphore()
    for other in (left, right):
        pl.semaphore_signal(barrier, inc=1, device_id=(other, side), device_id_type=MESH)
    for k in range(1, n_exp):
        pl.semaphore_signal(
            barrier, inc=1, device_id=(me, lax.rem(side + k, n_exp)), device_id_type=MESH
        )
    pl.semaphore_wait(barrier, 2 + n_exp - 1)

    def to_partner(k):
        return pltpu.make_async_remote_copy(
            src_ref=g_any,
            dst_ref=g_full.at[side],
            send_sem=send_g.at[k - 1],
            recv_sem=recv_g.at[k - 1],
            device_id=(me, lax.rem(side + k, n_exp)),
            device_id_type=MESH,
        )

    for k in range(1, n_exp):
        to_partner(k).start()
    mine = pltpu.make_async_copy(g_any, g_full.at[side], local_sem)
    mine.start()

    length, width = x_ref.shape
    heads = delta_t_ref.shape[1]
    tri = (iota((length, length), 0) >= iota((length, length), 1)).astype(F32)
    delta_t = delta_t_ref[...]
    logdecay = nn(tri, delta_t * rate_ref[...], HIGHEST)
    last = logdecay[length - 1 : length, :]
    grow = split(jnp.exp(logdecay), 3)
    keep = split(jnp.exp(last - logdecay) * delta_t, 2)
    b_t = b_t_ref[...].astype(BF16)
    c_t = c_t_ref[...].astype(BF16)

    @pl.loop(0, width // LANES)
    def _(i):
        lanes = pl.ds(pl.multiple_of(i * LANES, LANES), LANES)
        chosen = head_lanes(heads, LANES, i * (LANES // HEAD_DIM))
        grow_x = spread_out(grow, chosen)
        keep_x = spread_out(keep, chosen)
        own_f[:, lanes] = nn(b_t, (x_ref[:, lanes].astype(F32) * keep_x).astype(BF16))
        own_b[:, lanes] = nn(c_t, (g_ref[:, lanes].astype(F32) * grow_x).astype(BF16))
        through_ref[:, lanes] = jnp.broadcast_to(grow_x[length - 1 : length, :], (8, LANES))

    rows = own_f.shape[0] // pieces

    def hop(source, landing, send, recv, k, target):
        part = pl.ds(pl.multiple_of(k * rows, rows), rows)
        return pltpu.make_async_remote_copy(
            src_ref=source.at[part],
            dst_ref=landing.at[part],
            send_sem=send.at[k],
            recv_sem=recv.at[k],
            device_id=(target, side),
            device_id_type=MESH,
        )

    def handle(k, place, own, landing, outgoing, result, send, recv, target):
        part = pl.ds(pl.multiple_of(k * rows, rows), rows)

        @pl.when(place == 0)
        def _():
            result[part] = jnp.zeros((rows, width), F32)
            outgoing[part] = own[part]

        @pl.when(place > 0)
        def _():
            hop(outgoing, landing, send, recv, k, target).wait_recv()
            arrived = landing[part]
            result[part] = arrived
            outgoing[part] = through_ref[0:1, :] * arrived + own[part]

        @pl.when(place < n_ctx - 1)
        def _():
            hop(outgoing, landing, send, recv, k, target).start()

    back = n_ctx - 1 - me

    def lap(step, carry):
        k_f, k_b = step - me, step - back

        @pl.when((k_f >= 0) & (k_f < pieces))
        def _():
            handle(k_f, me, own_f, in_f, out_f, enter_ref, send_f, recv_f, right)

        @pl.when((k_b >= 0) & (k_b < pieces))
        def _():
            handle(k_b, back, own_b, in_b, out_b, leave_ref, send_b, recv_b, left)

        return carry

    lax.fori_loop(0, n_ctx - 1 + pieces, lap, 0)

    @pl.when(me < n_ctx - 1)
    def _():
        for k in range(pieces):
            hop(out_f, in_f, send_f, recv_f, k, right).wait_send()

    @pl.when(back < n_ctx - 1)
    def _():
        for k in range(pieces):
            hop(out_b, in_b, send_b, recv_b, k, left).wait_send()

    for k in range(1, n_exp):
        to_partner(k).wait_send()
    for k in range(1, n_exp):
        to_partner(k).wait_recv()
    mine.wait()


def scan_kernel(
    x_ref, g_ref, delta_ref, delta_t_ref, rate_row_ref, rate_col_ref, skip_ref,
    b_ref, c_ref, b_t_ref, c_t_ref, enter_ref, leave_ref,
    grad_x_ref, grad_delta_ref, grad_b_ref, grad_c_ref,
    log_row, gram_t, dgram_t, row_u, row_v,
):
    length, width = x_ref.shape
    heads = delta_ref.shape[0]
    chunks = length // CHUNK
    row_id, col_id = iota((length, length), 0), iota((length, length), 1)
    same = row_id // CHUNK == col_id // CHUNK
    lower = ((row_id >= col_id) & same).astype(F32)
    upper = ((row_id <= col_id) & same).astype(F32)
    delta, delta_t = delta_ref[...], delta_t_ref[...]
    log_rows = nn(delta * rate_col_ref[...], upper, HIGHEST)
    for h in range(heads):
        log_row[h] = log_rows[h : h + 1, :]
    log_t = nn(lower, delta_t * rate_row_ref[...], HIGHEST)
    ends = jnp.concatenate(
        [
            jnp.broadcast_to(log_t[(c + 1) * CHUNK - 1 : (c + 1) * CHUNK, :], (CHUNK, heads))
            for c in range(chunks)
        ],
        axis=0,
    )
    grow = split(jnp.exp(log_t), 2)
    keep = split(jnp.exp(ends - log_t) * delta_t, 2)
    offset = split(jnp.log(delta_t) - log_t, 3)
    for c in range(chunks):
        part = slice(c * CHUNK, (c + 1) * CHUNK)
        gram_t[part] = nt(b_ref[part], c_ref[part], HIGHEST)
    dgram_t[...] = jnp.zeros_like(dgram_t)
    row_u[...] = jnp.zeros_like(row_u)
    row_v[...] = jnp.zeros_like(row_v)
    grad_b_ref[...] = jnp.zeros_like(grad_b_ref)
    grad_c_ref[...] = jnp.zeros_like(grad_c_ref)
    causal = iota((CHUNK, CHUNK), 1) >= iota((CHUNK, CHUNK), 0)
    first_half = iota((CHUNK, LANES), 1) < HEAD_DIM
    last_row = iota((CHUNK, LANES), 0) == CHUNK - 1
    head_id = iota((heads, CHUNK), 0)
    per = LANES // HEAD_DIM

    @pl.loop(0, width // LANES)
    def _(i):
        lanes = pl.ds(pl.multiple_of(i * LANES, LANES), LANES)
        chosen = head_lanes(heads, LANES, i * per)
        grow_x = spread_out(grow, chosen)
        keep_x = spread_out(keep, chosen)
        columns = [
            spread_out(offset, (iota((heads, LANES), 0) == i * per + j).astype(BF16))
            for j in range(per)
        ]
        skip = skip_ref[0:1, lanes]
        parts = [slice(c * CHUNK, (c + 1) * CHUNK) for c in range(chunks)]
        xs = [x_ref[part, lanes] for part in parts]
        gs = [g_ref[part, lanes] for part in parts]
        kept = [(xs[c].astype(F32) * keep_x[parts[c]]).astype(BF16) for c in range(chunks)]
        grown = [(gs[c].astype(F32) * grow_x[parts[c]]).astype(BF16) for c in range(chunks)]
        through = [grow_x[(c + 1) * CHUNK - 1 : (c + 1) * CHUNK, :] for c in range(chunks)]
        states = [enter_ref[:, lanes]]
        for c in range(chunks):
            states.append(
                through[c] * states[c] + nn(b_t_ref[:, parts[c]].astype(BF16), kept[c])
            )
        grads = [None] * chunks + [leave_ref[:, lanes]]
        for c in reversed(range(chunks)):
            grads[c] = through[c] * grads[c + 1] + nn(c_t_ref[:, parts[c]].astype(BF16), grown[c])
        for c in range(chunks):
            part = parts[c]
            state, grad = states[c].astype(BF16), grads[c + 1].astype(BF16)
            from_grad = nn(b_ref[part].astype(BF16), grad) * keep_x[part]
            from_state = nn(c_ref[part].astype(BF16), state) * grow_x[part]
            grad_c_ref[part] += nt(grown[c], state)
            grad_b_ref[part] += nt(kept[c], grad)
            gram = gram_t[part]
            total = None
            within = []
            for j in range(per):
                mask = first_half if j == 0 else jnp.logical_not(first_half)
                x_half = jnp.where(mask, xs[c].astype(F32), 0.0).astype(BF16)
                pair = nt(x_half, gs[c])
                log_t_row = log_row[i * per + j, :, part]
                weight = jnp.exp(jnp.where(causal, log_t_row + columns[j][part], -1e30))
                value = weight * pair
                total = value if total is None else total + value
                summed = jnp.sum(value * gram, axis=0, keepdims=True)
                row_u[:, part] += jnp.where(head_id == i * per + j, summed, 0.0)
                within.append(nn((weight * gram).astype(BF16), gs[c]))
            dgram_t[part] += total
            inner = jnp.where(first_half, within[0], within[1]) + from_grad
            g_wide = gs[c].astype(F32)
            grad_x_ref[part, lanes] = (inner + skip * g_wide).astype(BF16)
            used = xs[c].astype(F32) * inner
            ending = jnp.sum(states[c + 1] * grads[c + 1], axis=0, keepdims=True)
            reached = g_wide * from_state + jnp.where(last_row, ending, 0.0)
            for piece in split(used, 2):
                row_v[:, part] += nt(chosen, piece)
            for piece in split(reached, 2):
                row_u[:, part] += nt(chosen, piece)

    drift = nn(row_u[...] - row_v[...], lower, HIGHEST)
    grad_delta_ref[...] = row_v[...] / delta + rate_col_ref[...] * drift
    for c in range(chunks):
        part = slice(c * CHUNK, (c + 1) * CHUNK)
        grad_b_ref[part] += nn(dgram_t[part], c_ref[part], HIGHEST)
        grad_c_ref[part] += nn(dgram_t[part].T, b_ref[part], HIGHEST)


def expert_kernel(
    n_exp,
    g_ref, ids_ref, probs_ref, w_ref, act_ref, b_any, c_any,
    grad_act_ref, grad_slots_ref, out_b, out_c,
    in_b, in_c, send_b, recv_b, send_c, recv_c,
):
    me, side = lax.axis_index("ctx"), lax.axis_index("exp")
    step, steps = pl.program_id(0), pl.num_programs(0)
    rows = out_b.shape[0]

    def hop(k, source, landing, send, recv):
        target = lax.rem(side + k, n_exp)
        return pltpu.make_async_remote_copy(
            src_ref=source.at[pl.ds(pl.multiple_of(target * rows, rows), rows)],
            dst_ref=landing.at[k - 1],
            send_sem=send.at[k - 1],
            recv_sem=recv.at[k - 1],
            device_id=(me, target),
            device_id_type=MESH,
        )

    @pl.when(step == 0)
    def _():
        barrier = pltpu.get_barrier_semaphore()
        for k in range(1, n_exp):
            pl.semaphore_signal(
                barrier, inc=1, device_id=(me, lax.rem(side + k, n_exp)), device_id_type=MESH
            )
        pl.semaphore_wait(barrier, n_exp - 1)
        for k in range(1, n_exp):
            hop(k, b_any, in_b, send_b, recv_b).start()
            hop(k, c_any, in_c, send_c, recv_c).start()

    length = ids_ref.shape[1]
    capacity = act_ref.shape[1]
    part_width = g_ref.shape[2]
    expert = side * steps + step
    named = ids_ref[...] == expert
    hit = jnp.sum(named.astype(F32), axis=0, keepdims=True)
    prob = jnp.sum(jnp.where(named, probs_ref[...], 0.0), axis=0, keepdims=True)
    before = (iota((length, length), 0) < iota((length, length), 1)).astype(BF16)
    rank = nn(jnp.broadcast_to(hit, (16, length)).astype(BF16), before)[0:1, :]
    place = jnp.where(hit > 0.5, rank, -1.0)
    picks = iota((capacity, length), 0).astype(F32) == place
    weight = jnp.sum(jnp.where(picks, prob, 0.0), axis=1, keepdims=True)
    chosen = picks.astype(BF16)
    inner = None
    for j in range(n_exp):
        picked = nn(chosen, g_ref[j]).astype(BF16)
        term = nt(picked, w_ref[0, :, j * part_width : (j + 1) * part_width])
        inner = term if inner is None else inner + term
    grad_act_ref[0] = (weight * inner).astype(BF16)
    product = act_ref[0].astype(F32) * inner
    ones = jnp.ones((16, product.shape[1]), BF16)
    summed = None
    for piece in split(product, 2):
        term = nt(ones, piece)
        summed = term if summed is None else summed + term
    grad_slots_ref[0] = summed[0:1, :]

    @pl.when(step == steps - 1)
    def _():
        mine = pl.ds(pl.multiple_of(side * rows, rows), rows)
        total_b, total_c = b_any[mine], c_any[mine]
        for k in range(1, n_exp):
            hop(k, b_any, in_b, send_b, recv_b).wait()
            hop(k, c_any, in_c, send_c, recv_c).wait()
            total_b = total_b + in_b[k - 1]
            total_c = total_c + in_c[k - 1]
        out_b[...] = total_b
        out_c[...] = total_c


def per_device(
    n_ctx, n_exp,
    feature_in, grad_out, delta, decay_log, skip_gain, b_proj, c_proj,
    route_ids, route_probs, w_down, saved_act,
):
    length, width = feature_in.shape
    heads = delta.shape[0]
    nstate = b_proj.shape[1]
    rate = -jnp.exp(decay_log)
    rate_row, rate_col = rate[None, :], rate[:, None]
    skip = jnp.repeat(skip_gain, HEAD_DIM)[None, :]
    delta_t, b_t, c_t = delta.T, b_proj.T, c_proj.T
    vmem = pl.BlockSpec(memory_space=pltpu.VMEM)
    hbm = pl.BlockSpec(memory_space=pl.ANY)
    state = jax.ShapeDtypeStruct((nstate, width), F32)
    pieces = nstate // 8
    others = n_exp - 1
    g_full, enter, leave = pl.pallas_call(
        partial(chain_kernel, n_ctx, n_exp, pieces),
        out_shape=(jax.ShapeDtypeStruct((n_exp, length, width), BF16), state, state),
        in_specs=[vmem, vmem, hbm, vmem, vmem, vmem, vmem],
        out_specs=(hbm, vmem, vmem),
        scratch_shapes=[pltpu.VMEM((nstate, width), F32)] * 6
        + [pltpu.VMEM((8, width), F32)]
        + [pltpu.SemaphoreType.DMA((pieces,))] * 4
        + [pltpu.SemaphoreType.DMA((others,))] * 2
        + [pltpu.SemaphoreType.DMA],
        compiler_params=pltpu.CompilerParams(
            collective_id=0, has_side_effects=True, vmem_limit_bytes=40 << 20
        ),
        name="state_chain",
    )(feature_in, grad_out, grad_out, delta_t, rate_row, b_t, c_t)

    square = jax.ShapeDtypeStruct((length, nstate), F32)
    grad_x, grad_delta, part_b, part_c = pl.pallas_call(
        scan_kernel,
        out_shape=(
            jax.ShapeDtypeStruct((length, width), BF16),
            jax.ShapeDtypeStruct((heads, length), F32),
            square,
            square,
        ),
        in_specs=[vmem] * 13,
        out_specs=(vmem,) * 4,
        scratch_shapes=[
            pltpu.VMEM((heads, 1, length), F32),
            pltpu.VMEM((length, CHUNK), F32),
            pltpu.VMEM((length, CHUNK), F32),
            pltpu.VMEM((heads, length), F32),
            pltpu.VMEM((heads, length), F32),
        ],
        compiler_params=pltpu.CompilerParams(vmem_limit_bytes=40 << 20),
        name="scan_grads",
    )(
        feature_in, grad_out, delta, delta_t, rate_row, rate_col, skip,
        b_proj, c_proj, b_t, c_t, enter, leave,
    )

    experts, hidden, full = w_down.shape
    capacity = saved_act.shape[2]
    rows = length // n_exp
    whole = lambda *shape: pl.BlockSpec(shape, lambda e: (0,) * len(shape))
    shard = jax.ShapeDtypeStruct((rows, nstate), F32)
    grad_act, grad_slots, grad_b, grad_c = pl.pallas_call(
        partial(expert_kernel, n_exp),
        grid=(experts,),
        out_shape=(
            jax.ShapeDtypeStruct((experts, capacity, hidden), BF16),
            jax.ShapeDtypeStruct((experts, 1, capacity), F32),
            shard,
            shard,
        ),
        in_specs=[
            whole(n_exp, length, width),
            whole(route_ids.shape[1], length),
            whole(route_ids.shape[1], length),
            pl.BlockSpec((1, hidden, full), lambda e: (e, 0, 0)),
            pl.BlockSpec((1, capacity, hidden), lambda e: (e, 0, 0)),
            vmem,
            vmem,
        ],
        out_specs=(
            pl.BlockSpec((1, capacity, hidden), lambda e: (e, 0, 0)),
            pl.BlockSpec((1, 1, capacity), lambda e: (e, 0, 0)),
            whole(rows, nstate),
            whole(rows, nstate),
        ),
        scratch_shapes=[pltpu.VMEM((others, rows, nstate), F32)] * 2
        + [pltpu.SemaphoreType.DMA((others,))] * 4,
        compiler_params=pltpu.CompilerParams(
            collective_id=1, has_side_effects=True, vmem_limit_bytes=40 << 20
        ),
        name="expert_grads",
    )(g_full, route_ids.T, route_probs.T, w_down, saved_act[0], part_b, part_c)
    return (grad_x, grad_delta, grad_b, grad_c, grad_act[None], grad_slots.reshape(1, experts, capacity))


def solution(mesh):
    placed = (
        P("ctx", "exp"),
        P("ctx", "exp"),
        P("exp", "ctx"),
        P("exp"),
        P("exp"),
        P("ctx", None),
        P("ctx", None),
        P("ctx", None),
        P("ctx", None),
        P("exp", None, None),
        P("ctx", "exp", None, None),
    )
    return jax.shard_map(
        partial(per_device, mesh.shape["ctx"], mesh.shape["exp"]),
        mesh=mesh,
        in_specs=placed,
        out_specs=(
            P("ctx", "exp"),
            P("exp", "ctx"),
            P(("ctx", "exp"), None),
            P(("ctx", "exp"), None),
            P("ctx", "exp", None, None),
            P("ctx", "exp", None),
        ),
        check_vma=False,
    )
```

time: 572 us -> 130 us (0.23); the launches traced: 565 us -> 129 us
  local copies, waits for them, and re-layouts: 141 us -> 9.52 us
  other arithmetic: 131 us -> 0.66 us
  matrix products: 121 us -> 0 us
  Pallas kernels: 0 us -> 118 us
  waiting for transfers between devices: 101 us -> 0 us
  blocking collectives: 36.4 us -> 0 us
  between operations: 15.1 us -> 0.73 us
  loops' own time: 12.9 us -> 0 us
  starting transfers between devices: 7.19 us -> 0 us
    dot_general x37 -> x0, matrix products: 121 us -> none  [the longest x6 31.5 us: block_step(): jnp.einsum('hts,ts,shp->thp', weights, gram_mat, driven, precision=HIGHEST)]
    pallas_call x0 -> x3, Pallas kernels: none -> 118 us  [the longest x1 77.5 us: per_device(): pl.pallas_call(partial(chain_kernel, n_ctx, n_exp, pieces), out_shape=(ja...]
    all_gather x2 -> x0, waiting for transfers between devices: 75.3 us -> none  [prefix(): pieces = jax.tree.map(lambda part: lax.all_gather(part, axis), value)]
    select_n x33 -> x0, other arithmetic: 43.9 us -> none  [the longest x30 43.9 us: lap(): jnp.where(position < mine, new, old)]
    unnamed x1 -> x0, blocking collectives: 36.4 us -> none
    dynamic_update_slice x18 -> x0, other arithmetic: 31 us -> none  [run_blocks(): lax.scan(block_fn, start_state, (x_blocks, d_blocks, b_blocks, c_blocks))]
    all_to_all x1 -> x0, waiting for transfers between devices: 25.1 us -> none  [per_device(): lax.all_to_all(padded[slot_table], 'exp', split_axis=0, concat_axis=2, ti...]
    dynamic_slice x19 -> x0, local copies, waits for them, and re-layouts: 22.3 us -> none  [the longest x18 21.7 us: run_blocks(): lax.scan(block_fn, start_state, (x_blocks, d_blocks, b_blocks, c_blocks))]
  transfers between devices with their start and end apart: 5 -> 0, of which waited for: 2 -> 0; matrix products, arithmetic and copies ran while one was open for 27% -> 0% of each run, Pallas kernels for 0% -> 0%
where the time goes in v1:
time: 130 us; the launch traced here: 129 us
  Pallas kernels  118 us (91%)
  local copies, waits for them, and re-layouts  9.52 us (7%)
    pallas_call x1, Pallas kernels, per_device(): pl.pallas_call(partial(chain_kernel, n_ctx, n_exp, pieces), out_shape=(ja...  77.5 us
    pallas_call x1, Pallas kernels, per_device(): pl.pallas_call(scan_kernel, out_shape=(jax.ShapeDtypeStruct((length, widt...  26.1 us
    pallas_call x1, Pallas kernels, per_device(): pl.pallas_call(partial(expert_kernel, n_exp), grid=(experts,), out_shape=...  14.8 us
    unnamed x23, local copies, waits for them, and re-layouts  8.62 us

profile of v1, /device:TPU:0, one launch (start us, length us, event | category | flops | bytes accessed | tf_op | source)
XLA Modules:
  0.0 129.3 jit_solution(3969644934777672532)
XLA Ops:
  0.6 0.7 fusion
  1.3 0.1 copy.20.rate_col_ref
  1.4 0.7 broadcast_in_dim.14
  2.1 0.1 broadcast_in_dim_reshape.3.skip_ref
  2.2 0.9 copy.17
  3.1 1.1 copy.18
  4.2 1.1 copy.19
  5.2 0.0 copy-start
  5.3 1.4 %copy-done = bf16[384,2048]{1,0:T(8,128)(2,1)S(1)} copy-done((bf16[384,2048]{1,0:T(8,128)(2,1)S(1)}, bf16[384,2048]{1,0:T(8,128)(2,1)}, u32[]{:S(2)}) %copy-start) | copy-done | bytes 1572888
  6.7 0.0 copy-start.1
  6.7 1.4 %copy-done.1 = bf16[384,2048]{1,0:T(8,128)(2,1)S(1)} copy-done((bf16[384,2048]{1,0:T(8,128)(2,1)S(1)}, bf16[384,2048]{1,0:T(8,128)(2,1)}, u32[]{:S(2)}) %copy-start.1) | copy-done | bytes 1572888
  8.1 0.0 copy-start.2
  8.1 0.0 copy-start.3
  8.1 0.0 copy-start.5
  8.1 77.5 %state_chain.1 = (bf16[2,384,2048]{2,1,0:T(8,128)(2,1)S(1)}, f32[128,2048]{1,0:T(8,128)S(1)}, f32[128,2048]{1,0:T(8,128)S(1)}) custom-call(bf16[384,2048]{1,0:T(8,128)(2,1)S(1)} %copy-done.1, bf16[384,2048]{1,0:T(8,128)(2,1)S(1)} %copy-done, bf16[384,2048]{1,0:T(8,128)(2,1)S(1)} %copy-done, f32[384,32]{1,0:T(8,128)S(1)} %bitcast.16, ...), custom_call_target="tpu_custom_call" | custom-call | tf_op jit(solution)/shard_map/state_chain/pallas_call | solution.py:373
  85.6 0.0 copy-done.2
  85.6 0.0 copy-done.3
  85.6 0.0 copy-done.5
  85.6 0.0 copy-start.4
  85.6 0.0 copy-start.6
  85.6 0.0 copy-start.7
  85.6 26.1 %scan_grads.1 = (bf16[384,2048]{1,0:T(8,128)(2,1)}, f32[32,384]{1,0:T(8,128)}, f32[384,128]{1,0:T(8,128)S(1)}, f32[384,128]{1,0:T(8,128)S(1)}) custom-call(bf16[384,2048]{1,0:T(8,128)(2,1)S(1)} %copy-done.1, bf16[384,2048]{1,0:T(8,128)(2,1)S(1)} %copy-done, f32[32,384]{1,0:T(8,128)S(1)} %copy-done.5, f32[384,32]{1,0:T(8,128)S(1)} %bitcast.17, ...), custom_call_target="tpu_custom_call" | custom-call | tf_op jit(solution)/shard_map/scan_grads/pallas_call | solution.py:390
  111.8 0.0 copy-done.4
  111.8 0.0 copy-done.6
  111.8 0.0 copy-done.7
  111.8 14.8 %expert_grads.1 = (bf16[4,240,384]{2,1,0:T(8,128)(2,1)S(1)}, f32[4,1,240]{2,1,0:T(1,128)S(1)}, f32[192,128]{1,0:T(8,128)S(1)}, f32[192,128]{1,0:T(8,128)S(1)}) custom-call(bf16[2,384,2048]{2,1,0:T(8,128)(2,1)S(1)} %get-tuple-element.21.g_ref, s32[4,384]{1,0:T(4,128)S(1)} %bitcast.20, f32[4,384]{1,0:T(4,128)S(1)} %bitcast.21, bf16[4,384,4096]{2,1,0:T(8,128)(2,1)} %w_ref.1, ...), custom_call_target="tpu_custom_call" | custom-call | tf_op jit(solution)/shard_map/expert_grads/pallas_call | solution.py:419
  126.6 0.6 copy.21
  127.2 0.6 copy.25
  127.8 0.6 copy.26
  128.4 0.9 copy.27
Async XLA Ops:
  5.2 1.4 %copy-start = (bf16[384,2048]{1,0:T(8,128)(2,1)S(1)}, bf16[384,2048]{1,0:T(8,128)(2,1)}, u32[]{:S(2)}) copy-start(bf16[384,2048]{1,0:T(8,128)(2,1)} %g_ref.3) | copy-start | bytes 4718596
  6.7 1.4 %copy-start.1 = (bf16[384,2048]{1,0:T(8,128)(2,1)S(1)}, bf16[384,2048]{1,0:T(8,128)(2,1)}, u32[]{:S(2)}) copy-start(bf16[384,2048]{1,0:T(8,128)(2,1)} %x_ref.3) | copy-start | bytes 4718596
  8.1 77.5 %copy-start.2 = (f32[384,128]{1,0:T(8,128)S(1)}, f32[384,128]{1,0:T(8,128)}, u32[]{:S(2)}) copy-start(f32[384,128]{1,0:T(8,128)} %b_ref.1) | copy-start | bytes 589828
  8.1 77.5 %copy-start.3 = (f32[384,128]{1,0:T(8,128)S(1)}, f32[384,128]{1,0:T(8,128)}, u32[]{:S(2)}) copy-start(f32[384,128]{1,0:T(8,128)} %c_ref.1) | copy-start | bytes 589828
  8.1 77.5 %copy-start.5 = (f32[32,384]{1,0:T(8,128)S(1)}, f32[32,384]{1,0:T(8,128)}, u32[]{:S(2)}) copy-start(f32[32,384]{1,0:T(8,128)} %delta_ref.1) | copy-start | bytes 147460
  85.6 26.1 %copy-start.4 = (bf16[1,4,240,384]{3,2,1,0:T(8,128)(2,1)S(1)}, bf16[1,4,240,384]{3,2,1,0:T(8,128)(2,1)}, u32[]{:S(2)}) copy-start(bf16[1,4,240,384]{3,2,1,0:T(8,128)(2,1)} %param.21) | copy-start | bytes 2211844
  85.6 26.1 %copy-start.6 = (s32[384,4]{0,1:T(4,128)S(1)}, s32[384,4]{0,1:T(4,128)}, u32[]{:S(2)}) copy-start(s32[384,4]{0,1:T(4,128)} %param.18) | copy-start | bytes 18436
  85.6 26.1 %copy-start.7 = (f32[384,4]{0,1:T(4,128)S(1)}, f32[384,4]{0,1:T(4,128)}, u32[]{:S(2)}) copy-start(f32[384,4]{0,1:T(4,128)} %param.19) | copy-start | bytes 18436

commit v2 on v1

v2 whole, which is shorter than its diff:
```python
from functools import partial

import jax
import jax.numpy as jnp
from jax import lax
from jax.experimental import pallas as pl
from jax.experimental.pallas import tpu as pltpu
from jax.sharding import PartitionSpec as P

HEAD_DIM = 64
CHUNK = 128
LANES = 128
HIGHEST = lax.Precision.HIGHEST
F32 = jnp.float32
BF16 = jnp.bfloat16
MESH = pl.DeviceIdType.MESH


def nn(a, b, precision=None):
    return lax.dot_general(
        a, b, (((1,), (0,)), ((), ())), precision=precision, preferred_element_type=F32
    )


def nt(a, b, precision=None):
    return lax.dot_general(
        a, b, (((1,), (1,)), ((), ())), precision=precision, preferred_element_type=F32
    )


def split(value, count):
    parts = []
    for _ in range(count):
        part = value.astype(BF16)
        parts.append(part)
        value = value - part.astype(F32)
    return parts


def spread_out(parts, chosen):
    total = nn(parts[0], chosen)
    for part in parts[1:]:
        total = total + nn(part, chosen)
    return total


def iota(shape, dim):
    return lax.broadcasted_iota(jnp.int32, shape, dim)


def head_lanes(heads, width, first):
    return (iota((heads, width), 0) == first + iota((heads, width), 1) // HEAD_DIM).astype(BF16)


def block_kernel(
    n_ctx, n_exp, pieces,
    x_ref, g_ref, delta_ref, delta_t_ref, rate_row_ref, rate_col_ref, skip_ref,
    b_ref, c_ref, b_t_ref, c_t_ref, ids_ref, probs_ref, act_ref, w_any,
    grad_x_ref, grad_delta_ref, grad_b_ref, grad_c_ref, grad_act_ref, grad_slots_ref,
    own_f, own_b, in_f, in_b, out_f, out_b, through_ref, g_in, w_ref,
    log_row, grow_hi, grow_lo, keep_hi, keep_lo, off_hi, off_mid, off_lo,
    gram_t, dgram_t, row_u, row_v, inside, part_b, part_c, land_b, land_c, act_sum,
    send_f, recv_f, send_b, recv_b, send_g, recv_g, load_w, send_p, recv_p, send_q, recv_q,
):
    me, side = lax.axis_index("ctx"), lax.axis_index("exp")
    right, left = lax.rem(me + 1, n_ctx), lax.rem(me + n_ctx - 1, n_ctx)
    barrier = pltpu.get_barrier_semaphore()
    for other in (left, right):
        pl.semaphore_signal(barrier, inc=1, device_id=(other, side), device_id_type=MESH)
    for k in range(1, n_exp):
        pl.semaphore_signal(
            barrier, inc=1, device_id=(me, lax.rem(side + k, n_exp)), device_id_type=MESH
        )
    pl.semaphore_wait(barrier, 2 + n_exp - 1)

    def to_partner(k):
        return pltpu.make_async_remote_copy(
            src_ref=g_ref,
            dst_ref=g_in.at[k - 1],
            send_sem=send_g.at[k - 1],
            recv_sem=recv_g.at[k - 1],
            device_id=(me, lax.rem(side + k, n_exp)),
            device_id_type=MESH,
        )

    for k in range(1, n_exp):
        to_partner(k).start()
    experts = w_ref.shape[0]

    def weights(e):
        return pltpu.make_async_copy(w_any.at[e], w_ref.at[e], load_w.at[e])

    for e in range(experts):
        weights(e).start()

    length, width = x_ref.shape
    heads = delta_t_ref.shape[1]
    chunks = length // CHUNK
    per = LANES // HEAD_DIM
    pairs = width // LANES
    delta, delta_t = delta_ref[...], delta_t_ref[...]
    row_id, col_id = iota((length, length), 0), iota((length, length), 1)
    same = row_id // CHUNK == col_id // CHUNK
    tri = (row_id >= col_id).astype(F32)
    lower = ((row_id >= col_id) & same).astype(F32)
    upper = ((row_id <= col_id) & same).astype(F32)
    pace = delta_t * rate_row_ref[...]

    shard_log = nn(tri, pace, HIGHEST)
    last = shard_log[length - 1 : length, :]
    shard_grow = split(jnp.exp(shard_log), 3)
    shard_keep = split(jnp.exp(last - shard_log) * delta_t, 2)
    b_t = b_t_ref[...].astype(BF16)
    c_t = c_t_ref[...].astype(BF16)

    @pl.loop(0, pairs)
    def _(i):
        lanes = pl.ds(pl.multiple_of(i * LANES, LANES), LANES)
        chosen = head_lanes(heads, LANES, i * per)
        grow_x = spread_out(shard_grow, chosen)
        keep_x = spread_out(shard_keep, chosen)
        own_f[:, lanes] = nn(b_t, (x_ref[:, lanes].astype(F32) * keep_x).astype(BF16))
        own_b[:, lanes] = nn(c_t, (g_ref[:, lanes].astype(F32) * grow_x).astype(BF16))
        through_ref[:, lanes] = jnp.broadcast_to(grow_x[length - 1 : length, :], (8, LANES))

    rows = own_f.shape[0] // pieces

    def hop(source, landing, send, recv, k, target):
        part = pl.ds(pl.multiple_of(k * rows, rows), rows)
        return pltpu.make_async_remote_copy(
            src_ref=source.at[part],
            dst_ref=landing.at[part],
            send_sem=send.at[k],
            recv_sem=recv.at[k],
            device_id=(target, side),
            device_id_type=MESH,
        )

    def handle(k, place, own, landing, outgoing, send, recv, target):
        part = pl.ds(pl.multiple_of(k * rows, rows), rows)

        @pl.when(place == 0)
        def _():
            landing[part] = jnp.zeros((rows, width), F32)
            outgoing[part] = own[part]

        @pl.when(place > 0)
        def _():
            hop(outgoing, landing, send, recv, k, target).wait_recv()
            outgoing[part] = through_ref[0:1, :] * landing[part] + own[part]

        @pl.when(place < n_ctx - 1)
        def _():
            hop(outgoing, landing, send, recv, k, target).start()

    back = n_ctx - 1 - me

    def chain_lap(step):
        k_f, k_b = step - me, step - back

        @pl.when((k_f >= 0) & (k_f < pieces))
        def _():
            handle(k_f, me, own_f, in_f, out_f, send_f, recv_f, right)

        @pl.when((k_b >= 0) & (k_b < pieces))
        def _():
            handle(k_b, back, own_b, in_b, out_b, send_b, recv_b, left)

    chain_lap(0)

    log_rows = nn(delta * rate_col_ref[...], upper, HIGHEST)
    for h in range(heads):
        log_row[h] = log_rows[h : h + 1, :]
    log_t = nn(lower, pace, HIGHEST)
    ends = jnp.concatenate(
        [
            jnp.broadcast_to(log_t[(c + 1) * CHUNK - 1 : (c + 1) * CHUNK, :], (CHUNK, heads))
            for c in range(chunks)
        ],
        axis=0,
    )
    grow_hi[...], grow_lo[...] = split(jnp.exp(log_t), 2)
    keep_hi[...], keep_lo[...] = split(jnp.exp(ends - log_t) * delta_t, 2)
    off_hi[...], off_mid[...], off_lo[...] = split(jnp.log(delta_t) - log_t, 3)
    for c in range(chunks):
        part = slice(c * CHUNK, (c + 1) * CHUNK)
        gram_t[part] = nt(b_ref[part], c_ref[part], HIGHEST)
    dgram_t[...] = jnp.zeros_like(dgram_t)
    row_u[...] = jnp.zeros_like(row_u)
    row_v[...] = jnp.zeros_like(row_v)
    causal = iota((CHUNK, CHUNK), 1) >= iota((CHUNK, CHUNK), 0)
    first_half = iota((CHUNK, LANES), 1) < HEAD_DIM
    last_row = iota((CHUNK, LANES), 0) == CHUNK - 1
    head_id = iota((heads, CHUNK), 0)
    parts = [slice(c * CHUNK, (c + 1) * CHUNK) for c in range(chunks)]

    def within_unit(i):
        lanes = pl.ds(pl.multiple_of(i * LANES, LANES), LANES)
        offset = [off_hi[...], off_mid[...], off_lo[...]]
        columns = [
            spread_out(offset, (iota((heads, LANES), 0) == i * per + j).astype(BF16))
            for j in range(per)
        ]
        for part in parts:
            x_part, g_part = x_ref[part, lanes], g_ref[part, lanes]
            gram = gram_t[part]
            total = None
            within = []
            for j in range(per):
                mask = first_half if j == 0 else jnp.logical_not(first_half)
                x_half = jnp.where(mask, x_part.astype(F32), 0.0).astype(BF16)
                pair = nt(x_half, g_part)
                log_t_row = log_row[i * per + j, :, part]
                weight = jnp.exp(jnp.where(causal, log_t_row + columns[j][part], -1e30))
                value = weight * pair
                total = value if total is None else total + value
                summed = jnp.sum(value * gram, axis=0, keepdims=True)
                row_u[:, part] += jnp.where(head_id == i * per + j, summed, 0.0)
                within.append(nn((weight * gram).astype(BF16), g_part))
            dgram_t[part] += total
            inside[part, lanes] = jnp.where(first_half, within[0], within[1])

    capacity = act_ref.shape[1]
    before = (row_id < col_id).astype(BF16)

    def expert_unit(e, k):
        named = ids_ref[...] == side * experts + e
        hit = jnp.sum(named.astype(F32), axis=0, keepdims=True)
        rank = nn(jnp.broadcast_to(hit, (16, length)).astype(BF16), before)[0:1, :]
        place = jnp.where(hit > 0.5, rank, -1.0)
        picks = iota((capacity, length), 0).astype(F32) == place
        chosen = picks.astype(BF16)
        owner = lax.rem(side + n_exp - k, n_exp)
        columns = pl.ds(pl.multiple_of(owner * width, width), width)

        def product(grad):
            picked = nn(chosen, grad).astype(BF16)
            return nt(picked, w_ref[e, :, columns])

        @pl.when(k == 0)
        def _():
            act_sum[...] = product(g_ref[...])

        @pl.when(k > 0)
        def _():
            act_sum[...] += product(g_in[lax.max(k - 1, 0)])

        @pl.when(k == n_exp - 1)
        def _():
            prob = jnp.sum(jnp.where(named, probs_ref[...], 0.0), axis=0, keepdims=True)
            weight = jnp.sum(jnp.where(picks, prob, 0.0), axis=1, keepdims=True)
            inner = act_sum[...]
            grad_act_ref[e] = (weight * inner).astype(BF16)
            scored = act_ref[e].astype(F32) * inner
            ones = jnp.ones((16, scored.shape[1]), BF16)
            summed = None
            for piece in split(scored, 2):
                term = nt(ones, piece)
                summed = term if summed is None else summed + term
            grad_slots_ref[e] = summed[0:1, :]

    units = experts * n_exp
    laps = max(n_ctx - 1 + pieces, pairs + 1 + units)

    def lap(step, carry):
        chain_lap(step)

        @pl.when(step <= pairs)
        def _():
            within_unit(step - 1)

        @pl.when(step == pairs)
        def _():
            for e in range(experts):
                weights(e).wait()
            for k in range(1, n_exp):
                to_partner(k).wait_send()
            for k in range(1, n_exp):
                to_partner(k).wait_recv()

        unit = step - pairs - 1

        @pl.when((unit >= 0) & (unit < units))
        def _():
            expert_unit(unit // n_exp, lax.rem(unit, n_exp))

        return carry

    lax.fori_loop(1, laps, lap, 0)

    @pl.when(me < n_ctx - 1)
    def _():
        for k in range(pieces):
            hop(out_f, in_f, send_f, recv_f, k, right).wait_send()

    @pl.when(back < n_ctx - 1)
    def _():
        for k in range(pieces):
            hop(out_b, in_b, send_b, recv_b, k, left).wait_send()

    for part in parts:
        part_b[part] = nn(dgram_t[part], c_ref[part], HIGHEST)
        part_c[part] = nn(dgram_t[part].T, b_ref[part], HIGHEST)

    @pl.loop(0, pairs)
    def _(i):
        lanes = pl.ds(pl.multiple_of(i * LANES, LANES), LANES)
        chosen = head_lanes(heads, LANES, i * per)
        grow_x = spread_out([grow_hi[...], grow_lo[...]], chosen)
        keep_x = spread_out([keep_hi[...], keep_lo[...]], chosen)
        skip = skip_ref[0:1, lanes]
        xs = [x_ref[part, lanes].astype(F32) for part in parts]
        gs = [g_ref[part, lanes].astype(F32) for part in parts]
        kept = [(xs[c] * keep_x[parts[c]]).astype(BF16) for c in range(chunks)]
        grown = [(gs[c] * grow_x[parts[c]]).astype(BF16) for c in range(chunks)]
        through = [grow_x[(c + 1) * CHUNK - 1 : (c + 1) * CHUNK, :] for c in range(chunks)]
        states = [in_f[:, lanes]]
        for c in range(chunks):
            states.append(
                through[c] * states[c] + nn(b_t_ref[:, parts[c]].astype(BF16), kept[c])
            )
        grads = [None] * chunks + [in_b[:, lanes]]
        for c in reversed(range(chunks)):
            grads[c] = through[c] * grads[c + 1] + nn(c_t_ref[:, parts[c]].astype(BF16), grown[c])
        for c in range(chunks):
            part = parts[c]
            state, grad = states[c].astype(BF16), grads[c + 1].astype(BF16)
            from_grad = nn(b_ref[part].astype(BF16), grad) * keep_x[part]
            from_state = nn(c_ref[part].astype(BF16), state) * grow_x[part]
            part_c[part] += nt(grown[c], state)
            part_b[part] += nt(kept[c], grad)
            inner = inside[part, lanes] + from_grad
            grad_x_ref[part, lanes] = (inner + skip * gs[c]).astype(BF16)
            used = xs[c] * inner
            ending = jnp.sum(states[c + 1] * grads[c + 1], axis=0, keepdims=True)
            reached = gs[c] * from_state + jnp.where(last_row, ending, 0.0)
            for piece in split(used, 2):
                row_v[:, part] += nt(chosen, piece)
            for piece in split(reached, 2):
                row_u[:, part] += nt(chosen, piece)

    share = grad_b_ref.shape[0]

    def shed(k, source, landing, send, recv):
        target = lax.rem(side + k, n_exp)
        return pltpu.make_async_remote_copy(
            src_ref=source.at[pl.ds(pl.multiple_of(target * share, share), share)],
            dst_ref=landing.at[k - 1],
            send_sem=send.at[k - 1],
            recv_sem=recv.at[k - 1],
            device_id=(me, target),
            device_id_type=MESH,
        )

    for k in range(1, n_exp):
        shed(k, part_b, land_b, send_p, recv_p).start()
        shed(k, part_c, land_c, send_q, recv_q).start()
    drift = nn(row_u[...] - row_v[...], lower, HIGHEST)
    grad_delta_ref[...] = row_v[...] / delta + rate_col_ref[...] * drift
    mine = pl.ds(pl.multiple_of(side * share, share), share)
    total_b, total_c = part_b[mine], part_c[mine]
    for k in range(1, n_exp):
        shed(k, part_b, land_b, send_p, recv_p).wait()
        shed(k, part_c, land_c, send_q, recv_q).wait()
        total_b = total_b + land_b[k - 1]
        total_c = total_c + land_c[k - 1]
    grad_b_ref[...] = total_b
    grad_c_ref[...] = total_c


def per_device(
    n_ctx, n_exp,
    feature_in, grad_out, delta, decay_log, skip_gain, b_proj, c_proj,
    route_ids, route_probs, w_down, saved_act,
):
    length, width = feature_in.shape
    heads = delta.shape[0]
    nstate = b_proj.shape[1]
    experts, hidden, full = w_down.shape
    capacity = saved_act.shape[2]
    share = length // n_exp
    others = n_exp - 1
    rate = -jnp.exp(decay_log)
    rate_row, rate_col = rate[None, :], rate[:, None]
    skip = jnp.repeat(skip_gain, HEAD_DIM)[None, :]
    vmem = pl.BlockSpec(memory_space=pltpu.VMEM)
    hbm = pl.BlockSpec(memory_space=pl.ANY)
    pieces = nstate // 8
    dma = pltpu.SemaphoreType.DMA
    shard = jax.ShapeDtypeStruct((share, nstate), F32)
    square = pltpu.VMEM((length, nstate), F32)
    by_head = pltpu.VMEM((heads, length), F32)
    grad_x, grad_delta, grad_b, grad_c, grad_act, grad_slots = pl.pallas_call(
        partial(block_kernel, n_ctx, n_exp, pieces),
        out_shape=(
            jax.ShapeDtypeStruct((length, width), BF16),
            jax.ShapeDtypeStruct((heads, length), F32),
            shard,
            shard,
            jax.ShapeDtypeStruct((experts, capacity, hidden), BF16),
            jax.ShapeDtypeStruct((experts, 1, capacity), F32),
        ),
        in_specs=[vmem] * 14 + [hbm],
        out_specs=(vmem,) * 6,
        scratch_shapes=[pltpu.VMEM((nstate, width), F32)] * 6
        + [pltpu.VMEM((8, width), F32)]
        + [pltpu.VMEM((others, length, width), BF16)]
        + [pltpu.VMEM((experts, hidden, full), BF16)]
        + [pltpu.VMEM((heads, 1, length), F32)]
        + [pltpu.VMEM((length, heads), BF16)] * 7
        + [pltpu.VMEM((length, CHUNK), F32)] * 2
        + [by_head] * 2
        + [pltpu.VMEM((length, width), F32)]
        + [square] * 2
        + [pltpu.VMEM((others, share, nstate), F32)] * 2
        + [pltpu.VMEM((capacity, hidden), F32)]
        + [dma((pieces,))] * 4
        + [dma((others,))] * 2
        + [dma((experts,))]
        + [dma((others,))] * 4,
        compiler_params=pltpu.CompilerParams(
            collective_id=0, has_side_effects=True, vmem_limit_bytes=50 << 20
        ),
        name="block_grads",
    )(
        feature_in, grad_out, delta, delta.T, rate_row, rate_col, skip,
        b_proj, c_proj, b_proj.T, c_proj.T, route_ids.T, route_probs.T, saved_act[0], w_down,
    )
    return (grad_x, grad_delta, grad_b, grad_c, grad_act[None], grad_slots.reshape(1, experts, capacity))


def solution(mesh):
    placed = (
        P("ctx", "exp"),
        P("ctx", "exp"),
        P("exp", "ctx"),
        P("exp"),
        P("exp"),
        P("ctx", None),
        P("ctx", None),
        P("ctx", None),
        P("ctx", None),
        P("exp", None, None),
        P("ctx", "exp", None, None),
    )
    return jax.shard_map(
        partial(per_device, mesh.shape["ctx"], mesh.shape["exp"]),
        mesh=mesh,
        in_specs=placed,
        out_specs=(
            P("ctx", "exp"),
            P("exp", "ctx"),
            P(("ctx", "exp"), None),
            P(("ctx", "exp"), None),
            P("ctx", "exp", None, None),
            P("ctx", "exp", None),
        ),
        check_vma=False,
    )
```

time: 130 us -> 126 us (0.969)
  Pallas kernels: 118 us -> 110 us
  local copies, waits for them, and re-layouts: 9.52 us -> 14.1 us
    pallas_call x3 -> x1, Pallas kernels: 118 us -> 110 us  [per_device(): pl.pallas_call(partial(block_kernel, n_ctx, n_exp, pieces), out_shape=(ja...]
    unnamed x23 -> x21, local copies, waits for them, and re-layouts: 8.62 us -> 13.2 us
where the time goes in v2:
time: 126 us; the launch traced here: 125 us
  Pallas kernels  110 us (87%)
  local copies, waits for them, and re-layouts  14.1 us (11%)
    pallas_call x1, Pallas kernels, per_device(): pl.pallas_call(partial(block_kernel, n_ctx, n_exp, pieces), out_shape=(ja...  110 us
    unnamed x21, local copies, waits for them, and re-layouts  13.2 us

profile of v2, /device:TPU:0, one launch (start us, length us, event | category | flops | bytes accessed | tf_op | source)
XLA Modules:
  0.0 125.2 jit_solution(85097577771815436)
XLA Ops:
  0.6 0.0 copy-start.2
  0.6 0.7 fusion
  1.4 0.1 copy.20.rate_col_ref
  1.5 0.7 broadcast_in_dim.14
  2.2 0.1 broadcast_in_dim_reshape.3.skip_ref
  2.3 0.9 copy.17
  3.2 1.1 copy.18
  4.3 1.1 copy.19
  5.3 0.0 copy-done.2
  5.3 0.0 copy-start
  5.3 0.9 copy-done
  6.3 0.0 copy-start.1
  6.3 0.9 copy-done.1
  7.2 0.0 copy-start.3
  7.2 0.8 copy-done.3
  8.0 0.0 copy-start.4
  8.0 0.7 copy-done.4
  8.7 0.0 copy-start.5
  8.7 0.7 copy-done.5
  9.4 109.8 %block_grads.1 = (bf16[384,2048]{1,0:T(8,128)(2,1)}, f32[32,384]{1,0:T(8,128)S(1)}, f32[192,128]{1,0:T(8,128)S(1)}, f32[192,128]{1,0:T(8,128)S(1)}, bf16[4,240,3...) custom-call(bf16[384,2048]{1,0:T(8,128)(2,1)} %x_ref.1, bf16[384,2048]{1,0:T(8,128)(2,1)} %g_ref.1, ...), custom_call_target="tpu_custom_call" | custom-call | tf_op jit(solution)/shard_map/block_grads/pallas_call | solution.py:393
  119.1 0.6 copy.21
  119.7 2.7 %copy.27 = bf16[384,2048]{1,0:T(8,128)(2,1)} copy(bf16[384,2048]{1,0:T(8,128)(2,1)} %get-tuple-element.32) | data formatting | bytes 3145728
  122.5 0.6 copy.28
  123.1 0.6 copy.29
  123.7 0.6 copy.30
  124.4 0.9 copy.31
Async XLA Ops:
  0.6 4.7 %copy-start.2 = (bf16[1,4,240,384]{3,2,1,0:T(8,128)(2,1)S(1)}, bf16[1,4,240,384]{3,2,1,0:T(8,128)(2,1)}, u32[]{:S(2)}) copy-start(bf16[1,4,240,384]{3,2,1,0:T(8,128)(2,1)} %param.21) | copy-start | bytes 2211844
  5.3 0.9 copy-start
  6.3 0.9 copy-start.1
  7.2 0.8 copy-start.3
  8.0 0.7 copy-start.4
  8.7 0.7 copy-start.5

commit v3 on v2

--- a/solution.py
+++ b/solution.py
@@ -10,6 +10,7 @@
 HEAD_DIM = 64
 CHUNK = 128
 LANES = 128
+HOP_LAPS = 2
 HIGHEST = lax.Precision.HIGHEST
 F32 = jnp.float32
 BF16 = jnp.bfloat16
@@ -55,11 +56,11 @@
 def block_kernel(
     n_ctx, n_exp, pieces,
     x_ref, g_ref, delta_ref, delta_t_ref, rate_row_ref, rate_col_ref, skip_ref,
-    b_ref, c_ref, b_t_ref, c_t_ref, ids_ref, probs_ref, act_ref, w_any,
+    b_ref, c_ref, ids_ref, probs_ref, act_ref, w_any,
     grad_x_ref, grad_delta_ref, grad_b_ref, grad_c_ref, grad_act_ref, grad_slots_ref,
     own_f, own_b, in_f, in_b, out_f, out_b, through_ref, g_in, w_ref,
     log_row, grow_hi, grow_lo, keep_hi, keep_lo, off_hi, off_mid, off_lo,
-    gram_t, dgram_t, row_u, row_v, inside, part_b, part_c, land_b, land_c, act_sum,
+    gram_t, dgram_t, row_u, row_v, inside, part_b, part_c, land_b, land_c, act_sum, b_t_ref, c_t_ref,
     send_f, recv_f, send_b, recv_b, send_g, recv_g, load_w, send_p, recv_p, send_q, recv_q,
 ):
     me, side = lax.axis_index("ctx"), lax.axis_index("exp")
@@ -108,10 +109,12 @@
 
     shard_log = nn(tri, pace, HIGHEST)
     last = shard_log[length - 1 : length, :]
-    shard_grow = split(jnp.exp(shard_log), 3)
+    shard_grow = split(jnp.exp(shard_log), 2)
     shard_keep = split(jnp.exp(last - shard_log) * delta_t, 2)
-    b_t = b_t_ref[...].astype(BF16)
-    c_t = c_t_ref[...].astype(BF16)
+    b_t = b_ref[...].T.astype(BF16)
+    c_t = c_ref[...].T.astype(BF16)
+    b_t_ref[...] = b_t
+    c_t_ref[...] = c_t
 
     @pl.loop(0, pairs)
     def _(i):
@@ -155,8 +158,13 @@
 
     back = n_ctx - 1 - me
 
+    def first_lap(place):
+        return (place + 1) // 2 + HOP_LAPS * (place // 2)
+
+    start_f, start_b = first_lap(me), first_lap(back)
+
     def chain_lap(step):
-        k_f, k_b = step - me, step - back
+        k_f, k_b = step - start_f, step - start_b
 
         @pl.when((k_f >= 0) & (k_f < pieces))
         def _():
@@ -260,7 +268,7 @@
             grad_slots_ref[e] = summed[0:1, :]
 
     units = experts * n_exp
-    laps = max(n_ctx - 1 + pieces, pairs + 1 + units)
+    laps = max(first_lap(n_ctx - 1) + pieces, pairs + 1 + units)
 
     def lap(step, carry):
         chain_lap(step)
@@ -317,11 +325,11 @@
         states = [in_f[:, lanes]]
         for c in range(chunks):
             states.append(
-                through[c] * states[c] + nn(b_t_ref[:, parts[c]].astype(BF16), kept[c])
+                through[c] * states[c] + nn(b_t_ref[:, parts[c]], kept[c])
             )
         grads = [None] * chunks + [in_b[:, lanes]]
         for c in reversed(range(chunks)):
-            grads[c] = through[c] * grads[c + 1] + nn(c_t_ref[:, parts[c]].astype(BF16), grown[c])
+            grads[c] = through[c] * grads[c + 1] + nn(c_t_ref[:, parts[c]], grown[c])
         for c in range(chunks):
             part = parts[c]
             state, grad = states[c].astype(BF16), grads[c + 1].astype(BF16)
@@ -385,7 +393,7 @@
     skip = jnp.repeat(skip_gain, HEAD_DIM)[None, :]
     vmem = pl.BlockSpec(memory_space=pltpu.VMEM)
     hbm = pl.BlockSpec(memory_space=pl.ANY)
-    pieces = nstate // 8
+    pieces = nstate // 16
     dma = pltpu.SemaphoreType.DMA
     shard = jax.ShapeDtypeStruct((share, nstate), F32)
     square = pltpu.VMEM((length, nstate), F32)
@@ -400,7 +408,7 @@
             jax.ShapeDtypeStruct((experts, capacity, hidden), BF16),
             jax.ShapeDtypeStruct((experts, 1, capacity), F32),
         ),
-        in_specs=[vmem] * 14 + [hbm],
+        in_specs=[vmem] * 12 + [hbm],
         out_specs=(vmem,) * 6,
         scratch_shapes=[pltpu.VMEM((nstate, width), F32)] * 6
         + [pltpu.VMEM((8, width), F32)]
@@ -414,6 +422,7 @@
         + [square] * 2
         + [pltpu.VMEM((others, share, nstate), F32)] * 2
         + [pltpu.VMEM((capacity, hidden), F32)]
+        + [pltpu.VMEM((nstate, length), BF16)] * 2
         + [dma((pieces,))] * 4
         + [dma((others,))] * 2
         + [dma((experts,))]
@@ -424,7 +433,7 @@
         name="block_grads",
     )(
         feature_in, grad_out, delta, delta.T, rate_row, rate_col, skip,
-        b_proj, c_proj, b_proj.T, c_proj.T, route_ids.T, route_probs.T, saved_act[0], w_down,
+        b_proj, c_proj, route_ids.T, route_probs.T, saved_act[0], w_down,
     )
     return (grad_x, grad_delta, grad_b, grad_c, grad_act[None], grad_slots.reshape(1, experts, capacity))
 

time: 126 us -> 108 us (0.86)
  Pallas kernels: 110 us -> 95.1 us
  local copies, waits for them, and re-layouts: 14.1 us -> 11.5 us
    pallas_call x1, Pallas kernels: 110 us -> 95.1 us  [per_device(): pl.pallas_call(partial(block_kernel, n_ctx, n_exp, pieces), out_shape=(ja...]
    unnamed x21 -> x19, local copies, waits for them, and re-layouts: 13.2 us -> 10.6 us
where the time goes in v3:
time: 108 us
  Pallas kernels  95.1 us (88%)
  local copies, waits for them, and re-layouts  11.5 us (11%)
    pallas_call x1, Pallas kernels, per_device(): pl.pallas_call(partial(block_kernel, n_ctx, n_exp, pieces), out_shape=(ja...  95.1 us
    unnamed x19, local copies, waits for them, and re-layouts  10.6 us

profile of v3, /device:TPU:0, one launch (start us, length us, event | category | flops | bytes accessed | tf_op | source)
XLA Modules:
  0.0 107.9 jit_solution(1762441698385486350)
XLA Ops:
  0.6 0.7 fusion
  1.3 0.1 copy.18.rate_col_ref
  1.4 0.7 broadcast_in_dim.14
  2.1 0.1 broadcast_in_dim_reshape.3.skip_ref
  2.2 0.9 copy.17
  3.1 0.0 copy-start
  3.1 1.1 %copy-done = bf16[1,4,240,384]{3,2,1,0:T(8,128)(2,1)S(1)} copy-done((bf16[1,4,240,384]{3,2,1,0:T(8,128)(2,1)S(1)}, bf16[1,4,240,384]{3,2,1,0:T(8,128)(2,1)}, u32[]{:S(2)}) %copy-start) | copy-done | bytes 737304
  4.2 0.0 copy-start.1
  4.2 0.9 copy-done.1
  5.2 0.0 copy-start.2
  5.2 0.9 copy-done.2
  6.1 0.0 copy-start.3
  6.1 0.8 copy-done.3
  6.9 0.0 copy-start.4
  6.9 0.7 copy-done.4
  7.6 0.0 copy-start.5
  7.6 0.7 copy-done.5
  8.3 95.1 %block_grads.1 = (bf16[384,2048]{1,0:T(8,128)(2,1)S(1)}, f32[32,384]{1,0:T(8,128)S(1)}, f32[192,128]{1,0:T(8,128)S(1)}, f32[192,128]{1,0:T(8,128)S(1)}, bf16[4,2...) custom-call(bf16[384,2048]{1,0:T(8,128)(2,1)} %x_ref.1, bf16[384,2048]{1,0:T(8,128)(2,1)} %g_ref.1, ...), custom_call_target="tpu_custom_call" | custom-call | tf_op jit(solution)/shard_map/block_grads/pallas_call | solution.py:401
  103.4 0.6 copy.19
  104.0 1.1 %copy.25 = bf16[384,2048]{1,0:T(8,128)(2,1)} copy(bf16[384,2048]{1,0:T(8,128)(2,1)S(1)} %get-tuple-element.32) | data formatting | bytes 3145728
  105.1 0.6 copy.26
  105.8 0.6 copy.27
  106.4 0.6 copy.28
  107.0 0.9 copy.29
Async XLA Ops:
  3.1 1.1 %copy-start = (bf16[1,4,240,384]{3,2,1,0:T(8,128)(2,1)S(1)}, bf16[1,4,240,384]{3,2,1,0:T(8,128)(2,1)}, u32[]{:S(2)}) copy-start(bf16[1,4,240,384]{3,2,1,0:T(8,128)(2,1)} %param.21) | copy-start | bytes 2211844
  4.2 0.9 copy-start.1
  5.2 0.9 copy-start.2
  6.1 0.8 copy-start.3
  6.9 0.7 copy-start.4
  7.6 0.7 copy-start.5
